TPU v7x, 512 devices: a whole 4x4x16 slice. The times are simulated.
512 devices in a mesh: lat: 16 (over x, y_lo, core), lon: 32 (over y_hi, z).
Axes of the slice: x: 4, y: 4 (y_hi: 2, y_lo: 2; y = y_hi * 2 + y_lo), z: 16, core: 2. Of those that a mesh axis runs over, the one named last changes fastest.
Arguments:
- features: bfloat16 [64, 1024, 256], P('lat', 'lon'), may hold values from -6 to 6
- cotangent: bfloat16 [64, 1024, 256], P('lat', 'lon'), may hold values from -6 to 6
- weight: bfloat16 [4, 256, 256], replicated, may hold values from -0.1875 to 0.1875
- filter_taps: bfloat16 [64, 4, 5, 64], P('lat'), may hold values from -6 to 6
- lat_ext: int32 [64], P('lat'), may hold values from 1 to 3, as said below
- lon_count: int32 [64], P('lat'), may hold values from 1 to 32, as said below
Outputs:
- output: bfloat16 [64, 1024, 256], P('lat', 'lon')
- field_grad: bfloat16 [64, 1024, 256], P('lat', 'lon')
- weight_grad: float32 [4, 256, 256], replicated
Inputs may be any that keep to these rules, and one draw needn't show every extreme that they name: `lat_ext`: a row uses the latitude offsets whose magnitude is below its entry. `lon_count`: a row uses the longitude offsets whose magnitude is below its entry.
All inputs are finite; a program needn't handle non-finite values.
Results may differ from a plain program's by a relative error of at most 0.006.
Values may be sent and summed in bfloat16 or wider, within the bound.
A program may use at most 64 MiB of HBM per device.

v0:
```python
import math

import jax
import jax.numpy as jnp
from jax import lax
from jax.sharding import PartitionSpec as P


def extended(cells, sides, width, closed):
    for axis, dim in sides:
        count = lax.axis_size(axis)
        ends = count if closed else count - 1
        head = lax.slice_in_dim(cells, 0, width, axis=dim)
        tail = lax.slice_in_dim(cells, cells.shape[dim] - width, cells.shape[dim], axis=dim)
        cells = jnp.concatenate(
            [
                lax.ppermute(tail, axis, [(i, (i + 1) % count) for i in range(ends)]),
                cells,
                lax.ppermute(head, axis, [((i + 1) % count, i) for i in range(ends)]),
            ],
            axis=dim,
        )
    return cells


def make_filters(filter_taps, lat_ext, lon_count):
    lat_reach = filter_taps.shape[2] // 2
    half_width = filter_taps.shape[3] // 2
    lat_dist = jnp.abs(jnp.arange(filter_taps.shape[2], dtype=jnp.int32) - lat_reach)
    lon_dist = jnp.abs(jnp.arange(filter_taps.shape[3], dtype=jnp.int32) - half_width)
    support = (lat_dist[None, :, None] < lat_ext[:, None, None]) & (
        lon_dist[None, None, :] < lon_count[:, None, None]
    )
    support_size = ((2 * lat_ext - 1) * (2 * lon_count - 1)).astype(jnp.float32)
    row_scale = lax.rsqrt(support_size)
    masked = (
        filter_taps.astype(jnp.float32)
        * support[:, None].astype(jnp.float32)
        * row_scale[:, None, None, None]
    )
    return masked.astype(jnp.bfloat16)


def forward_taps(row_taps, lon_width):
    leading = row_taps.shape[:-1]
    return jnp.concatenate(
        [row_taps, jnp.zeros(leading + (lon_width + 1,), row_taps.dtype)], axis=-1
    )


def reverse_taps(row_taps, lon_width):
    leading = row_taps.shape[:-1]
    return jnp.concatenate(
        [
            jnp.zeros(leading + (1,), row_taps.dtype),
            row_taps[..., ::-1],
            jnp.zeros(leading + (lon_width,), row_taps.dtype),
        ],
        axis=-1,
    )


def band_matrix(padded, lon_width):
    leading = padded.shape[:-1]
    repeated = jnp.tile(padded, (1,) * len(leading) + (lon_width,))
    return repeated[..., : lon_width * 3 * lon_width].reshape(leading + (lon_width, 3 * lon_width))


def gather_adjoint(filter_rims, basis_rows, row_count, lon_width, channels, basis_count, lat_taps):
    last = lat_taps - 1
    diagonal = jnp.stack(
        [
            filter_rims[last - offset : last - offset + row_count, :, offset]
            for offset in range(lat_taps)
        ],
        axis=2,
    )
    banded = band_matrix(reverse_taps(diagonal, lon_width), lon_width)
    total_grad = jnp.zeros((row_count, lon_width, channels), jnp.float32)
    for basis_index in range(basis_count):
        grad_window = basis_rows(basis_index)
        patches = jnp.stack(
            [grad_window[last - offset : last - offset + row_count] for offset in range(lat_taps)],
            axis=1,
        )
        total_grad = total_grad + jnp.einsum(
            "oejn,oenc->ojc", banded[:, basis_index], patches, preferred_element_type=jnp.float32
        )
    return total_grad


def per_device(features, cotangent, weight, filter_taps, lat_ext, lon_count):
    row_count, lon_width, channels = features.shape
    basis_count = weight.shape[0]
    lat_taps = filter_taps.shape[2]
    lat_reach = lat_taps // 2
    filters = make_filters(filter_taps, lat_ext, lon_count)
    band_rows = extended(features, (("lat", 0),), lat_reach, False)
    window = extended(band_rows, (("lon", 1),), lon_width, True)
    banded_all = band_matrix(forward_taps(filters, lon_width), lon_width)
    patches = jnp.stack([window[offset : offset + row_count] for offset in range(lat_taps)], axis=1)
    basis_f32 = jnp.einsum(
        "okejm,oemc->ojkc", banded_all, patches, preferred_element_type=jnp.float32
    )
    basis_out = basis_f32.astype(jnp.bfloat16)
    flat_out = basis_out.reshape(row_count * lon_width, basis_count * channels)
    flat_weight = weight.reshape(basis_count * channels, channels)
    output = jnp.dot(flat_out, flat_weight, preferred_element_type=jnp.float32).astype(jnp.bfloat16)
    output = output.reshape(row_count, lon_width, channels)
    flat_cot = cotangent.reshape(row_count * lon_width, channels)
    partial_grad = lax.dot_general(
        flat_out, flat_cot, (((0,), (0,)), ((), ())), preferred_element_type=jnp.float32
    )
    total_cells = row_count * lax.axis_size("lat") * lon_width * lax.axis_size("lon")
    summed_grad = lax.psum(partial_grad, ("lat", "lon"))
    weight_grad = (summed_grad * (1.0 / math.sqrt(total_cells))).reshape(
        basis_count, channels, channels
    )
    filter_rims = extended(filters, (("lat", 0),), lat_reach, False)

    def received_rows(basis_index):
        own_grad = lax.dot_general(
            flat_cot,
            weight[basis_index],
            (((1,), (1,)), ((), ())),
            preferred_element_type=jnp.float32,
        ).astype(jnp.bfloat16)
        own_grad = own_grad.reshape(row_count, lon_width, channels)
        grad_band = extended(own_grad, (("lat", 0),), lat_reach, False)
        return extended(grad_band, (("lon", 1),), lon_width, True)

    field_grad = gather_adjoint(
        filter_rims, received_rows, row_count, lon_width, channels, basis_count, lat_taps
    ).astype(jnp.bfloat16)
    return (output, field_grad, weight_grad)


def solution(mesh):
    in_specs = (
        P("lat", "lon", None),
        P("lat", "lon", None),
        P(),
        P("lat", None, None, None),
        P("lat"),
        P("lat"),
    )
    out_specs = (P("lat", "lon", None), P("lat", "lon", None), P())
    return jax.shard_map(
        per_device, mesh=mesh, in_specs=in_specs, out_specs=out_specs, check_vma=False
    )
```

profile of v0, /device:TPU:1, one launch (start us, length us, event | category | flops | bytes accessed | tf_op | source)
XLA Modules:
  0.0 597.4 jit_solution(2804473898359303226)
XLA Ops:
  7.2 0.8 copy-done
  8.0 1.1 convolution_convert_fusion.4
  9.1 0.6 fusion.43
  9.7 4.6 collective-permute-start.6
  14.3 5.5 collective-permute-start.7
  19.8 0.7 broadcast_compare_fusion
  20.5 0.7 convert_rsqrt_fusion
  21.2 0.7 broadcast_compare_fusion.1
  22.0 0.8 multiply_convert_fusion
  22.8 1.9 collective-permute-start.4
  24.8 3.6 collective-permute-start.5
  28.4 0.2 convolution_convert_fusion.3
  28.6 0.6 fusion.42
  29.3 1.9 collective-permute-start.10
  31.2 0.2 convolution_convert_fusion.2
  31.4 0.2 convolution_convert_fusion.1
  31.6 0.6 fusion.41
  32.2 0.8 copy-done.8
  33.0 0.6 fusion.44
  33.8 0.1 tile.8
  33.9 1.8 tile.9
  35.7 0.2 slice.249
  35.9 0.5 reshape.131
  36.4 2.4 collective-permute-start.11
  38.9 3.2 collective-permute-start.14
  42.1 0.1 rev.3
  42.2 0.1 maximum_maximum_fusion
  42.3 0.1 tile.20
  42.4 1.8 tile.21
  44.2 0.2 slice.253
  44.4 0.5 reshape.135
  44.9 0.2 copy-done.10
  45.1 1.9 collective-permute-start.15
  47.0 3.6 collective-permute-start.18
  50.7 1.9 collective-permute-start.19
  52.7 3.6 collective-permute-start
  56.4 1.0 collective-permute-done
  57.3 1.9 collective-permute-start.1
  59.3 1.9 collective-permute-start.8
  61.2 10.9 %collective-permute-start.9 = (bf16[8,32,256]{2,1,0:T(8,128)(2,1)S(1)}, bf16[8,32,256]{2,1,0:T(8,128)(2,1)S(1)}, u32[]{:S(2)}, u32[]{:S(2)}) collective-permute-start(bf16[8,32,256]{2,1,0:T(8,128)(2,1)S(1)} %pad_maximum_fusion.5), channel_id=1, source_target_pairs={{1,0},{2,1},{3,2},{4,3},{5,4},{6,5},{7,6},{8,7},{9,8},{10,9},{11,1... | collective-permute-start | bytes 393224 | tf_op jit(solution)/shard_map/ppermute | solution.py:19
  72.2 1.9 collective-permute-start.12
  74.1 7.0 %collective-permute-start.13 = (bf16[8,32,256]{2,1,0:T(8,128)(2,1)S(1)}, bf16[8,32,256]{2,1,0:T(8,128)(2,1)S(1)}, u32[]{:S(2)}, u32[]{:S(2)}) collective-permute-start(bf16[8,32,256]{2,1,0:T(8,128)(2,1)S(1)} %pad_maximum_fusion.6), channel_id=1, source_target_pairs={{1,0},{2,1},{3,2},{4,3},{5,4},{6,5},{7,6},{8,7},{9,8},{10,9},{11,1... | collective-permute-start | bytes 393224 | tf_op jit(solution)/shard_map/ppermute | solution.py:19
  81.1 1.9 collective-permute-start.16
  83.1 7.0 %collective-permute-start.17 = (bf16[8,32,256]{2,1,0:T(8,128)(2,1)S(1)}, bf16[8,32,256]{2,1,0:T(8,128)(2,1)S(1)}, u32[]{:S(2)}, u32[]{:S(2)}) collective-permute-start(bf16[8,32,256]{2,1,0:T(8,128)(2,1)S(1)} %pad_maximum_fusion.7), channel_id=1, source_target_pairs={{1,0},{2,1},{3,2},{4,3},{5,4},{6,5},{7,6},{8,7},{9,8},{10,9},{11,1... | collective-permute-start | bytes 393224 | tf_op jit(solution)/shard_map/ppermute | solution.py:19
  90.1 1.9 collective-permute-start.20
  92.1 7.0 %collective-permute-start.21 = (bf16[8,32,256]{2,1,0:T(8,128)(2,1)S(1)}, bf16[8,32,256]{2,1,0:T(8,128)(2,1)S(1)}, u32[]{:S(2)}, u32[]{:S(2)}) collective-permute-start(bf16[8,32,256]{2,1,0:T(8,128)(2,1)S(1)} %pad_maximum_fusion.8), channel_id=1, source_target_pairs={{1,0},{2,1},{3,2},{4,3},{5,4},{6,5},{7,6},{8,7},{9,8},{10,9},{11,1... | collective-permute-start | bytes 393224 | tf_op jit(solution)/shard_map/ppermute | solution.py:19
  99.1 1.9 collective-permute-start.2
  101.2 7.0 %collective-permute-start.3 = (bf16[8,32,256]{2,1,0:T(8,128)(2,1)S(1)}, bf16[8,32,256]{2,1,0:T(8,128)(2,1)S(1)}, u32[]{:S(2)}, u32[]{:S(2)}) collective-permute-start(bf16[8,32,256]{2,1,0:T(8,128)(2,1)S(1)} %constant_dynamic-update-slice_fusion), channel_id=1, source_target_pairs={{1,0},{2,1},{3,2},{4,3},{5,4},{6,5},{7,6},{8,7},{9,8},{10,9},{11,1... | collective-permute-start | bytes 393224 | tf_op jit(solution)/shard_map/ppermute | solution.py:19
  108.4 0.9 copy-done.4
  109.5 0.3 collective-permute-done.2
  109.8 0.6 copy-done.6
  110.4 0.4 collective-permute-done.3
  111.0 0.4 fusion.1
  111.3 0.2 copy.36
  111.6 1.3 fusion.46
  112.9 0.9 convolution_convert_fusion
  113.8 0.3 convolution_bitcast_fusion.4
  114.1 0.3 fusion.4
  114.5 0.6 copy-done.7
  115.1 0.3 copy-done.5
  115.4 0.3 fusion.3
  115.7 1.0 fusion.5
  116.7 471.6 %all-reduce.3.cloned.1.call-done = f32[1024,256]{1,0:T(8,128)} async-done(((f32[1024,256]{1,0:T(8,128)}), f32[1024,256]{1,0:T(8,128)}) %all-reduce.3.cloned.1.call-update) | async-done | bytes 1048592 | tf_op jit(solution)/shard_map/psum | solution.py:115
  588.3 2.3 broadcast_multiply_fusion
  (90 shorter events, 1.1 us)
Async XLA Ops:
  7.2 0.8 copy-start
  7.2 21.2 %copy-start.1 = (bf16[4,256,256]{2,1,0:T(8,128)(2,1)S(1)}, bf16[4,256,256]{2,1,0:T(8,128)(2,1)}, u32[]{:S(2)}) copy-start(bf16[4,256,256]{2,1,0:T(8,128)(2,1)} %param.8) | copy-start | bytes 1572868
  7.2 581.1 %all-reduce.3.cloned.1.call-start = ((), (), s32[]{:S(2)}) async-start(), calls=%async_computation | async-start | bytes 2097152 | tf_op jit(solution)/shard_map/psum | solution.py:115
  9.7 35.1 %collective-permute-start.6 = (bf16[2,32,256]{2,1,0:T(8,128)(2,1)}, bf16[2,32,256]{2,1,0:T(8,128)(2,1)S(1)}, u32[]{:S(2)}, u32[]{:S(2)}) collective-permute-start(bf16[2,32,256]{2,1,0:T(8,128)(2,1)} %bitcast.19), channel_id=1, source_target_pairs={{0,32},{32,64},{64,96},{96,128},{128,160},{160,192},{192,224},{224... | collective-permute-start | bytes 98312 | tf_op jit(solution)/shard_map/ppermute | solution.py:17
  14.3 32.7 %collective-permute-start.7 = (bf16[2,32,256]{2,1,0:T(8,128)(2,1)}, bf16[2,32,256]{2,1,0:T(8,128)(2,1)S(1)}, u32[]{:S(2)}, u32[]{:S(2)}) collective-permute-start(bf16[2,32,256]{2,1,0:T(8,128)(2,1)} %bitcast.21), channel_id=1, source_target_pairs={{32,0},{64,32},{96,64},{128,96},{160,128},{192,160},{224,192},{256... | collective-permute-start | bytes 98312 | tf_op jit(solution)/shard_map/ppermute | solution.py:19
  22.8 13.5 %collective-permute-start.4 = (bf16[2,4,5,64]{3,1,2,0:T(4,128)(2,1)S(1)}, bf16[2,4,5,64]{3,1,2,0:T(4,128)(2,1)S(1)}, u32[]{:S(2)}, u32[]{:S(2)}) collective-permute-start(bf16[2,4,5,64]{3,1,2,0:T(4,128)(2,1)S(1)} %get-tuple-element.14), channel_id=1, source_target_pairs={{32,0},{64,32},{96,64},{128,96},{160,128},{192,160},{224,192},{256... | collective-permute-start | bytes 15368 | tf_op jit(solution)/shard_map/ppermute | solution.py:19
  24.8 14.1 %collective-permute-start.5 = (bf16[2,4,5,64]{3,1,2,0:T(4,128)(2,1)S(1)}, bf16[2,4,5,64]{3,1,2,0:T(4,128)(2,1)S(1)}, u32[]{:S(2)}, u32[]{:S(2)}) collective-permute-start(bf16[2,4,5,64]{3,1,2,0:T(4,128)(2,1)S(1)} %get-tuple-element.13), channel_id=1, source_target_pairs={{0,32},{32,64},{64,96},{96,128},{128,160},{160,192},{192,224},{224... | collective-permute-start | bytes 15368 | tf_op jit(solution)/shard_map/ppermute | solution.py:17
  29.3 21.5 %collective-permute-start.10 = (bf16[2,32,256]{2,1,0:T(8,128)(2,1)}, bf16[2,32,256]{2,1,0:T(8,128)(2,1)S(1)}, u32[]{:S(2)}, u32[]{:S(2)}) collective-permute-start(bf16[2,32,256]{2,1,0:T(8,128)(2,1)} %bitcast.35), channel_id=1, source_target_pairs={{0,32},{32,64},{64,96},{96,128},{128,160},{160,192},{192,224},{224... | collective-permute-start | bytes 98312 | tf_op jit(solution)/shard_map/ppermute | solution.py:17
  32.2 0.8 copy-start.8
  36.4 16.3 %collective-permute-start.11 = (bf16[2,32,256]{2,1,0:T(8,128)(2,1)}, bf16[2,32,256]{2,1,0:T(8,128)(2,1)S(1)}, u32[]{:S(2)}, u32[]{:S(2)}) collective-permute-start(bf16[2,32,256]{2,1,0:T(8,128)(2,1)} %bitcast.37), channel_id=1, source_target_pairs={{32,0},{64,32},{96,64},{128,96},{160,128},{192,160},{224,192},{256... | collective-permute-start | bytes 98312 | tf_op jit(solution)/shard_map/ppermute | solution.py:19
  38.9 20.4 %collective-permute-start.14 = (bf16[2,32,256]{2,1,0:T(8,128)(2,1)}, bf16[2,32,256]{2,1,0:T(8,128)(2,1)S(1)}, u32[]{:S(2)}, u32[]{:S(2)}) collective-permute-start(bf16[2,32,256]{2,1,0:T(8,128)(2,1)} %bitcast.51), channel_id=1, source_target_pairs={{0,32},{32,64},{64,96},{96,128},{128,160},{160,192},{192,224},{224... | collective-permute-start | bytes 98312 | tf_op jit(solution)/shard_map/ppermute | solution.py:17
  44.4 0.8 copy-start.10
  45.1 16.1 %collective-permute-start.15 = (bf16[2,32,256]{2,1,0:T(8,128)(2,1)S(1)}, bf16[2,32,256]{2,1,0:T(8,128)(2,1)S(1)}, u32[]{:S(2)}, u32[]{:S(2)}) collective-permute-start(bf16[2,32,256]{2,1,0:T(8,128)(2,1)S(1)} %bitcast.276), channel_id=1, source_target_pairs={{32,0},{64,32},{96,64},{128,96},{160,128},{192,160},{224,192},{256... | collective-permute-start | bytes 98312 | tf_op jit(solution)/shard_map/ppermute | solution.py:19
  47.0 27.1 %collective-permute-start.18 = (bf16[2,32,256]{2,1,0:T(8,128)(2,1)S(1)}, bf16[2,32,256]{2,1,0:T(8,128)(2,1)S(1)}, u32[]{:S(2)}, u32[]{:S(2)}) collective-permute-start(bf16[2,32,256]{2,1,0:T(8,128)(2,1)S(1)} %bitcast.275), channel_id=1, source_target_pairs={{0,32},{32,64},{64,96},{96,128},{128,160},{160,192},{192,224},{224... | collective-permute-start | bytes 98312 | tf_op jit(solution)/shard_map/ppermute | solution.py:17
  50.7 2.0 copy-start.11
  50.7 30.4 %collective-permute-start.19 = (bf16[2,32,256]{2,1,0:T(8,128)(2,1)S(1)}, bf16[2,32,256]{2,1,0:T(8,128)(2,1)S(1)}, u32[]{:S(2)}, u32[]{:S(2)}) collective-permute-start(bf16[2,32,256]{2,1,0:T(8,128)(2,1)S(1)} %bitcast.274), channel_id=1, source_target_pairs={{32,0},{64,32},{96,64},{128,96},{160,128},{192,160},{224,192},{256... | collective-permute-start | bytes 98312 | tf_op jit(solution)/shard_map/ppermute | solution.py:19
  52.7 4.7 collective-permute-start
  56.3 1.0 copy-start.9
  57.3 14.8 %collective-permute-start.1 = (bf16[2,32,256]{2,1,0:T(8,128)(2,1)S(1)}, bf16[2,32,256]{2,1,0:T(8,128)(2,1)S(1)}, u32[]{:S(2)}, u32[]{:S(2)}) collective-permute-start(bf16[2,32,256]{2,1,0:T(8,128)(2,1)S(1)} %copy-done.9), channel_id=1, source_target_pairs={{32,0},{64,32},{96,64},{128,96},{160,128},{192,160},{224,192},{256... | collective-permute-start | bytes 98312 | tf_op jit(solution)/shard_map/ppermute | solution.py:19
  59.3 23.8 %collective-permute-start.8 = (bf16[8,32,256]{2,1,0:T(8,128)(2,1)S(1)}, bf16[8,32,256]{2,1,0:T(8,128)(2,1)S(1)}, u32[]{:S(2)}, u32[]{:S(2)}) collective-permute-start(bf16[8,32,256]{2,1,0:T(8,128)(2,1)S(1)} %pad_maximum_fusion.5), channel_id=1, source_target_pairs={{0,1},{1,2},{2,3},{3,4},{4,5},{5,6},{6,7},{7,8},{8,9},{9,10},{10,1... | collective-permute-start | bytes 393224 | tf_op jit(solution)/shard_map/ppermute | solution.py:17
  61.2 28.8 %collective-permute-start.9 = (bf16[8,32,256]{2,1,0:T(8,128)(2,1)S(1)}, bf16[8,32,256]{2,1,0:T(8,128)(2,1)S(1)}, u32[]{:S(2)}, u32[]{:S(2)}) collective-permute-start(bf16[8,32,256]{2,1,0:T(8,128)(2,1)S(1)} %pad_maximum_fusion.5), channel_id=1, source_target_pairs={{1,0},{2,1},{3,2},{4,3},{5,4},{6,5},{7,6},{8,7},{9,8},{10,9},{11,1... | collective-permute-start | bytes 393224 | tf_op jit(solution)/shard_map/ppermute | solution.py:19
  72.2 20.0 %collective-permute-start.12 = (bf16[8,32,256]{2,1,0:T(8,128)(2,1)S(1)}, bf16[8,32,256]{2,1,0:T(8,128)(2,1)S(1)}, u32[]{:S(2)}, u32[]{:S(2)}) collective-permute-start(bf16[8,32,256]{2,1,0:T(8,128)(2,1)S(1)} %pad_maximum_fusion.6), channel_id=1, source_target_pairs={{0,1},{1,2},{2,3},{3,4},{4,5},{5,6},{6,7},{7,8},{8,9},{9,10},{10,1... | collective-permute-start | bytes 393224 | tf_op jit(solution)/shard_map/ppermute | solution.py:17
  74.1 25.0 %collective-permute-start.13 = (bf16[8,32,256]{2,1,0:T(8,128)(2,1)S(1)}, bf16[8,32,256]{2,1,0:T(8,128)(2,1)S(1)}, u32[]{:S(2)}, u32[]{:S(2)}) collective-permute-start(bf16[8,32,256]{2,1,0:T(8,128)(2,1)S(1)} %pad_maximum_fusion.6), channel_id=1, source_target_pairs={{1,0},{2,1},{3,2},{4,3},{5,4},{6,5},{7,6},{8,7},{9,8},{10,9},{11,1... | collective-permute-start | bytes 393224 | tf_op jit(solution)/shard_map/ppermute | solution.py:19
  81.1 20.1 %collective-permute-start.16 = (bf16[8,32,256]{2,1,0:T(8,128)(2,1)S(1)}, bf16[8,32,256]{2,1,0:T(8,128)(2,1)S(1)}, u32[]{:S(2)}, u32[]{:S(2)}) collective-permute-start(bf16[8,32,256]{2,1,0:T(8,128)(2,1)S(1)} %pad_maximum_fusion.7), channel_id=1, source_target_pairs={{0,1},{1,2},{2,3},{3,4},{4,5},{5,6},{6,7},{7,8},{8,9},{9,10},{10,1... | collective-permute-start | bytes 393224 | tf_op jit(solution)/shard_map/ppermute | solution.py:17
  83.1 25.2 %collective-permute-start.17 = (bf16[8,32,256]{2,1,0:T(8,128)(2,1)S(1)}, bf16[8,32,256]{2,1,0:T(8,128)(2,1)S(1)}, u32[]{:S(2)}, u32[]{:S(2)}) collective-permute-start(bf16[8,32,256]{2,1,0:T(8,128)(2,1)S(1)} %pad_maximum_fusion.7), channel_id=1, source_target_pairs={{1,0},{2,1},{3,2},{4,3},{5,4},{6,5},{7,6},{8,7},{9,8},{10,9},{11,1... | collective-permute-start | bytes 393224 | tf_op jit(solution)/shard_map/ppermute | solution.py:19
  90.1 18.4 %collective-permute-start.20 = (bf16[8,32,256]{2,1,0:T(8,128)(2,1)S(1)}, bf16[8,32,256]{2,1,0:T(8,128)(2,1)S(1)}, u32[]{:S(2)}, u32[]{:S(2)}) collective-permute-start(bf16[8,32,256]{2,1,0:T(8,128)(2,1)S(1)} %pad_maximum_fusion.8), channel_id=1, source_target_pairs={{0,1},{1,2},{2,3},{3,4},{4,5},{5,6},{6,7},{7,8},{8,9},{9,10},{10,1... | collective-permute-start | bytes 393224 | tf_op jit(solution)/shard_map/ppermute | solution.py:17
  92.1 17.2 %collective-permute-start.21 = (bf16[8,32,256]{2,1,0:T(8,128)(2,1)S(1)}, bf16[8,32,256]{2,1,0:T(8,128)(2,1)S(1)}, u32[]{:S(2)}, u32[]{:S(2)}) collective-permute-start(bf16[8,32,256]{2,1,0:T(8,128)(2,1)S(1)} %pad_maximum_fusion.8), channel_id=1, source_target_pairs={{1,0},{2,1},{3,2},{4,3},{5,4},{6,5},{7,6},{8,7},{9,8},{10,9},{11,1... | collective-permute-start | bytes 393224 | tf_op jit(solution)/shard_map/ppermute | solution.py:19
  99.1 10.6 %collective-permute-start.2 = (bf16[8,32,256]{2,1,0:T(8,128)(2,1)S(1)}, bf16[8,32,256]{2,1,0:T(8,128)(2,1)S(1)}, u32[]{:S(2)}, u32[]{:S(2)}) collective-permute-start(bf16[8,32,256]{2,1,0:T(8,128)(2,1)S(1)} %constant_dynamic-update-slice_fusion), channel_id=1, source_target_pairs={{0,1},{1,2},{2,3},{3,4},{4,5},{5,6},{6,7},{7,8},{8,9},{9,10},{10,1... | collective-permute-start | bytes 393224 | tf_op jit(solution)/shard_map/ppermute | solution.py:17
  101.2 7.0 %copy-start.2 = (bf16[4,5,96,256]{3,2,1,0:T(8,128)(2,1)}, bf16[4,5,96,256]{3,2,1,0:T(8,128)(2,1)S(1)}, u32[]{:S(2)}) copy-start(bf16[4,5,96,256]{3,2,1,0:T(8,128)(2,1)S(1)} %fusion.17) | copy-start | bytes 2949124
  101.2 9.6 %collective-permute-start.3 = (bf16[8,32,256]{2,1,0:T(8,128)(2,1)S(1)}, bf16[8,32,256]{2,1,0:T(8,128)(2,1)S(1)}, u32[]{:S(2)}, u32[]{:S(2)}) collective-permute-start(bf16[8,32,256]{2,1,0:T(8,128)(2,1)S(1)} %constant_dynamic-update-slice_fusion), channel_id=1, source_target_pairs={{1,0},{2,1},{3,2},{4,3},{5,4},{6,5},{7,6},{8,7},{9,8},{10,9},{11,1... | collective-permute-start | bytes 393224 | tf_op jit(solution)/shard_map/ppermute | solution.py:19
  108.4 0.9 copy-start.4
  109.5 0.9 copy-start.6
  112.9 1.2 copy-start.3
  113.8 1.3 copy-start.7
  114.1 1.3 copy-start.5
Sparse Core Ops, SparseCore 0:
  113.0 475.2 all-reduce.2
where the time goes:
time: 598 us; the launch traced here: 597 us
  waiting for transfers between devices  473 us (79%)
  starting transfers between devices  84.5 us (14%)
  between operations  14.9 us (2%)
  local copies, waits for them, and re-layouts  12.9 us (2%)
  matrix products  6.08 us (1%)
    psum x1, waiting for transfers between devices, per_device(): summed_grad = lax.psum(partial_grad, ('lat', 'lon'))  472 us
    ppermute x11, starting transfers between devices, extended(): lax.ppermute(head, axis, [((i + 1) % count, i) for i in range(ends)])  54.3 us
    ppermute x11, starting transfers between devices, extended(): lax.ppermute(tail, axis, [(i, (i + 1) % count) for i in range(ends)])  30.2 us
  transfers between devices with their start and end apart: 23, of which 4 were waited for; matrix products, arithmetic and copies ran while one was open for 2% of the time, Pallas kernels for 0%

commit v1 on v0

--- a/solution.py
+++ b/solution.py
@@ -3,7 +3,14 @@
 import jax
 import jax.numpy as jnp
 from jax import lax
+from jax.experimental import pallas as pl
+from jax.experimental.pallas import tpu as pltpu
 from jax.sharding import PartitionSpec as P
+
+MESH = pl.DeviceIdType.MESH
+PLANE = 16
+ZLEN = 16
+CHUNK = 32
 
 
 def extended(cells, sides, width, closed):
@@ -89,16 +96,185 @@
     return total_grad
 
 
+def sum_kernel(
+    part_ref, out_ref, pair_out, pair_in, half, plane_in, zbuf,
+    pair_sem, plane_send, plane_recv, z_send, z_recv, all_send, all_recv, near_send, near_recv,
+):
+    lat = lax.axis_index("lat")
+    lon = lax.axis_index("lon")
+    core = lat % 2
+    y_lo = (lat // 2) % 2
+    x = lat // 4
+    z = lon % ZLEN
+    y_hi = lon // ZLEN
+    spot = x * 4 + y_hi * 2 + y_lo
+    partner = (lat + 1 - 2 * core, lon)
+    rows = PLANE * CHUNK
+
+    def plane_device(index):
+        return ((index // 4) * 4 + (index % 2) * 2 + core, ((index // 2) % 2) * ZLEN + z)
+
+    def z_device(index):
+        return (lat, y_hi * ZLEN + index)
+
+    barrier = pltpu.get_barrier_semaphore()
+    pl.semaphore_signal(barrier, inc=1, device_id=partner, device_id_type=MESH)
+
+    def greet(step, carry):
+        pl.semaphore_signal(
+            barrier, inc=1, device_id=z_device((z + step) % ZLEN), device_id_type=MESH
+        )
+        pl.semaphore_signal(
+            barrier, inc=1, device_id=plane_device((spot + step) % PLANE), device_id_type=MESH
+        )
+        return carry
+
+    lax.fori_loop(1, PLANE, greet, 0)
+    theirs = pl.multiple_of((1 - core) * rows, rows)
+    mine = pl.multiple_of(core * rows, rows)
+    pair_out[...] = part_ref[pl.ds(theirs, rows), :].astype(jnp.bfloat16)
+    pl.semaphore_wait(barrier, 1 + (PLANE - 1) + (ZLEN - 1))
+
+    pair = pltpu.make_async_remote_copy(
+        src_ref=pair_out, dst_ref=pair_in, send_sem=pair_sem.at[0], recv_sem=pair_sem.at[1],
+        device_id=partner, device_id_type=MESH,
+    )
+    pair.start()
+    pair.wait()
+    total = part_ref[pl.ds(mine, rows), :] + pair_in[...].astype(jnp.float32)
+    half[...] = total.astype(jnp.bfloat16).reshape(PLANE, CHUNK, total.shape[-1])
+
+    def plane_copy(step):
+        target = (spot + step) % PLANE
+        return pltpu.make_async_remote_copy(
+            src_ref=half.at[target], dst_ref=plane_in.at[step], send_sem=plane_send.at[step],
+            recv_sem=plane_recv.at[step], device_id=plane_device(target), device_id_type=MESH,
+        )
+
+    def plane_start(step, carry):
+        plane_copy(step).start()
+        return carry
+
+    def plane_add(step, carry):
+        plane_copy(step).wait_recv()
+        return carry + plane_in[step].astype(jnp.float32)
+
+    lax.fori_loop(1, PLANE, plane_start, 0)
+    acc = lax.fori_loop(1, PLANE, plane_add, half[spot].astype(jnp.float32))
+    zbuf[z] = acc.astype(jnp.bfloat16)
+
+    def z_copy(step):
+        return pltpu.make_async_remote_copy(
+            src_ref=zbuf.at[z], dst_ref=zbuf.at[z], send_sem=z_send.at[step],
+            recv_sem=z_recv.at[z], device_id=z_device((z + step) % ZLEN), device_id_type=MESH,
+        )
+
+    def z_start(step, carry):
+        z_copy(step).start()
+        return carry
+
+    def z_wait(step, carry):
+        source = (z + step) % ZLEN
+        pltpu.make_async_remote_copy(
+            src_ref=zbuf.at[source], dst_ref=zbuf.at[source], send_sem=z_send.at[step],
+            recv_sem=z_recv.at[source], device_id=z_device(source), device_id_type=MESH,
+        ).wait_recv()
+        return carry
+
+    lax.fori_loop(1, ZLEN, z_start, 0)
+    lax.fori_loop(1, ZLEN, z_wait, 0)
+    acc = zbuf[0].astype(jnp.float32)
+    for source in range(1, ZLEN):
+        acc = acc + zbuf[source].astype(jnp.float32)
+    out_ref[core, spot] = acc.astype(jnp.bfloat16)
+
+    def all_copy(step):
+        return pltpu.make_async_remote_copy(
+            src_ref=out_ref.at[core, spot], dst_ref=out_ref.at[core, spot],
+            send_sem=all_send.at[step], recv_sem=all_recv.at[spot],
+            device_id=plane_device((spot + step) % PLANE), device_id_type=MESH,
+        )
+
+    def near_copy(index):
+        return pltpu.make_async_remote_copy(
+            src_ref=out_ref.at[core, index], dst_ref=out_ref.at[core, index],
+            send_sem=near_send.at[index], recv_sem=near_recv.at[index],
+            device_id=partner, device_id_type=MESH,
+        )
+
+    def all_start(step, carry):
+        all_copy(step).start()
+        return carry
+
+    def all_forward(step, carry):
+        source = (spot + step) % PLANE
+        pltpu.make_async_remote_copy(
+            src_ref=out_ref.at[core, source], dst_ref=out_ref.at[core, source],
+            send_sem=all_send.at[step], recv_sem=all_recv.at[source],
+            device_id=plane_device(source), device_id_type=MESH,
+        ).wait_recv()
+        near_copy(source).start()
+        return carry
+
+    lax.fori_loop(1, PLANE, all_start, 0)
+    near_copy(spot).start()
+    lax.fori_loop(1, PLANE, all_forward, 0)
+
+    def finish(step, carry):
+        plane_copy(step).wait_send()
+        z_copy(step).wait_send()
+        all_copy(step).wait_send()
+        return carry
+
+    lax.fori_loop(1, PLANE, finish, 0)
+
+    def near_finish(index, carry):
+        near_copy(index).wait_send()
+        pltpu.make_async_remote_copy(
+            src_ref=out_ref.at[1 - core, index], dst_ref=out_ref.at[1 - core, index],
+            send_sem=near_send.at[index], recv_sem=near_recv.at[index],
+            device_id=partner, device_id_type=MESH,
+        ).wait_recv()
+        return carry
+
+    lax.fori_loop(0, PLANE, near_finish, 0)
+
+
+def sum_all(partial_grad):
+    width = partial_grad.shape[1]
+    bf16 = jnp.bfloat16
+    dma = pltpu.SemaphoreType.DMA
+    return pl.pallas_call(
+        sum_kernel,
+        out_shape=jax.ShapeDtypeStruct((2, PLANE, CHUNK, width), bf16),
+        in_specs=[pl.BlockSpec(memory_space=pltpu.VMEM)],
+        out_specs=pl.BlockSpec(memory_space=pltpu.VMEM),
+        scratch_shapes=[
+            pltpu.VMEM((PLANE * CHUNK, width), bf16),
+            pltpu.VMEM((PLANE * CHUNK, width), bf16),
+            pltpu.VMEM((PLANE, CHUNK, width), bf16),
+            pltpu.VMEM((PLANE, CHUNK, width), bf16),
+            pltpu.VMEM((ZLEN, CHUNK, width), bf16),
+            dma((2,)), dma((PLANE,)), dma((PLANE,)), dma((ZLEN,)), dma((ZLEN,)),
+            dma((PLANE,)), dma((PLANE,)), dma((PLANE,)), dma((PLANE,)),
+        ],
+        compiler_params=pltpu.CompilerParams(collective_id=0, has_side_effects=True),
+    )(partial_grad)
+
+
 def per_device(features, cotangent, weight, filter_taps, lat_ext, lon_count):
     row_count, lon_width, channels = features.shape
     basis_count = weight.shape[0]
     lat_taps = filter_taps.shape[2]
     lat_reach = lat_taps // 2
     filters = make_filters(filter_taps, lat_ext, lon_count)
-    band_rows = extended(features, (("lat", 0),), lat_reach, False)
+    both = jnp.concatenate([features, cotangent], axis=-1)
+    band_rows = extended(both, (("lat", 0),), lat_reach, False)
     window = extended(band_rows, (("lon", 1),), lon_width, True)
     banded_all = band_matrix(forward_taps(filters, lon_width), lon_width)
-    patches = jnp.stack([window[offset : offset + row_count] for offset in range(lat_taps)], axis=1)
+    patches = jnp.stack(
+        [window[offset : offset + row_count, :, :channels] for offset in range(lat_taps)], axis=1
+    )
     basis_f32 = jnp.einsum(
         "okejm,oemc->ojkc", banded_all, patches, preferred_element_type=jnp.float32
     )
@@ -112,22 +288,21 @@
         flat_out, flat_cot, (((0,), (0,)), ((), ())), preferred_element_type=jnp.float32
     )
     total_cells = row_count * lax.axis_size("lat") * lon_width * lax.axis_size("lon")
-    summed_grad = lax.psum(partial_grad, ("lat", "lon"))
+    summed_grad = sum_all(partial_grad).astype(jnp.float32)
     weight_grad = (summed_grad * (1.0 / math.sqrt(total_cells))).reshape(
         basis_count, channels, channels
     )
     filter_rims = extended(filters, (("lat", 0),), lat_reach, False)
+    flat_window = window[..., channels:].reshape(-1, channels)
 
     def received_rows(basis_index):
-        own_grad = lax.dot_general(
-            flat_cot,
+        grad = lax.dot_general(
+            flat_window,
             weight[basis_index],
             (((1,), (1,)), ((), ())),
             preferred_element_type=jnp.float32,
         ).astype(jnp.bfloat16)
-        own_grad = own_grad.reshape(row_count, lon_width, channels)
-        grad_band = extended(own_grad, (("lat", 0),), lat_reach, False)
-        return extended(grad_band, (("lon", 1),), lon_width, True)
+        return grad.reshape(row_count + 2 * lat_reach, 3 * lon_width, channels)
 
     field_grad = gather_adjoint(
         filter_rims, received_rows, row_count, lon_width, channels, basis_count, lat_taps

time: 598 us -> 105 us (0.18)
  waiting for transfers between devices: 473 us -> 7.82 us
  starting transfers between devices: 84.5 us -> 26.6 us
  Pallas kernels: 0 us -> 43.2 us
  between operations: 14.9 us -> 1.19 us
    psum x1 -> x0, waiting for transfers between devices: 472 us -> none  [per_device(): summed_grad = lax.psum(partial_grad, ('lat', 'lon'))]
    pallas_call x0 -> x1, Pallas kernels: none -> 43.2 us  [sum_all(): pl.pallas_call(sum_kernel, out_shape=jax.ShapeDtypeStruct((2, PLANE, CHUN...]
    ppermute x11 -> x3, starting transfers between devices: 54.3 us -> 19.1 us  [extended(): lax.ppermute(head, axis, [((i + 1) % count, i) for i in range(ends)])]
    ppermute x11 -> x3, starting transfers between devices: 30.2 us -> 7.48 us  [extended(): lax.ppermute(tail, axis, [(i, (i + 1) % count) for i in range(ends)])]
    ppermute x11 -> x3, waiting for transfers between devices: 1.28 us -> 7.46 us  [extended(): lax.ppermute(tail, axis, [(i, (i + 1) % count) for i in range(ends)])]
  transfers between devices with their start and end apart: 23 -> 6, of which waited for: 4 -> 2; matrix products, arithmetic and copies ran while one was open for 2% -> 7% of each run, Pallas kernels for 0% -> 0%
where the time goes in v1:
time: 105 us
  Pallas kernels  43.2 us (41%)
  starting transfers between devices  26.6 us (25%)
  local copies, waits for them, and re-layouts  14.7 us (14%)
  waiting for transfers between devices  7.82 us (7%)
  matrix products  5.58 us (5%)
  other arithmetic  5.49 us (5%)
  between operations  1.19 us (1%)
    pallas_call x1, Pallas kernels, sum_all(): pl.pallas_call(sum_kernel, out_shape=jax.ShapeDtypeStruct((2, PLANE, CHUN...  43.2 us
    ppermute x3, starting transfers between devices, extended(): lax.ppermute(head, axis, [((i + 1) % count, i) for i in range(ends)])  19.1 us
    ppermute x3, starting transfers between devices, extended(): lax.ppermute(tail, axis, [(i, (i + 1) % count) for i in range(ends)])  7.48 us
    ppermute x3, waiting for transfers between devices, extended(): lax.ppermute(tail, axis, [(i, (i + 1) % count) for i in range(ends)])  7.46 us
    unnamed x53, local copies, waits for them, and re-layouts  5.22 us
    another operation x4, local copies, waits for them, and re-layouts, band_matrix(): repeated = jnp.tile(padded, (1,) * len(leading) + (lon_width,))  3.81 us
    slice x4, local copies, waits for them, and re-layouts, gather_adjoint(): grad_window[last - offset:last - offset + row_count]  2.88 us
    mul x1, other arithmetic, per_device(): summed_grad * (1.0 / math.sqrt(total_cells))  2.23 us
  transfers between devices with their start and end apart: 6, of which 2 were waited for; matrix products, arithmetic and copies ran while one was open for 7% of the time, Pallas kernels for 0%

profile of v1, /device:TPU:1, one launch (start us, length us, event | category | flops | bytes accessed | tf_op | source)
XLA Modules:
  0.0 104.5 jit_solution(15709654690906168955)
XLA Ops:
  0.7 0.7 convert_rsqrt_fusion
  1.3 0.7 broadcast_compare_fusion
  2.1 0.7 broadcast_compare_fusion.1
  2.8 0.1 and_convert_fusion
  2.9 0.8 multiply_convert_fusion
  3.7 8.7 %collective-permute-start.4 = (bf16[2,4,5,64]{3,1,2,0:T(4,128)(2,1)S(1)}, bf16[2,4,5,64]{3,1,2,0:T(4,128)(2,1)S(1)}, u32[]{:S(2)}, u32[]{:S(2)}) collective-permute-start(bf16[2,4,5,64]{3,1,2,0:T(4,128)(2,1)S(1)} %get-tuple-element.26), channel_id=1, source_target_pairs={{32,0},{64,32},{96,64},{128,96},{160,128},{192,160},{224,192},{256... | collective-permute-start | bytes 15368 | tf_op jit(solution)/shard_map/ppermute | solution.py:26
  12.4 0.8 constant_dynamic-update-slice_fusion.1
  13.3 0.8 constant_dynamic-update-slice_fusion
  14.1 1.9 %collective-permute-start.1 = (bf16[2,32,512]{2,1,0:T(8,128)(2,1)S(1)}, bf16[2,32,512]{2,1,0:T(8,128)(2,1)S(1)}, u32[]{:S(2)}, u32[]{:S(2)}) collective-permute-start(bf16[2,32,512]{2,1,0:T(8,128)(2,1)S(1)} %get-tuple-element.24), channel_id=1, source_target_pairs={{32,0},{64,32},{96,64},{128,96},{160,128},{192,160},{224,192},{256... | collective-permute-start | bytes 196616 | tf_op jit(solution)/shard_map/ppermute | solution.py:26
  16.1 3.6 %collective-permute-start = (bf16[2,32,512]{2,1,0:T(8,128)(2,1)S(1)}, bf16[2,32,512]{2,1,0:T(8,128)(2,1)S(1)}, u32[]{:S(2)}, u32[]{:S(2)}) collective-permute-start(bf16[2,32,512]{2,1,0:T(8,128)(2,1)S(1)} %get-tuple-element.23), channel_id=1, source_target_pairs={{0,32},{32,64},{64,96},{96,128},{128,160},{160,192},{192,224},{224... | collective-permute-start | bytes 196616 | tf_op jit(solution)/shard_map/ppermute | solution.py:24
  19.7 1.9 %collective-permute-start.5 = (bf16[2,4,5,64]{3,1,2,0:T(4,128)(2,1)S(1)}, bf16[2,4,5,64]{3,1,2,0:T(4,128)(2,1)S(1)}, u32[]{:S(2)}, u32[]{:S(2)}) collective-permute-start(bf16[2,4,5,64]{3,1,2,0:T(4,128)(2,1)S(1)} %get-tuple-element.25), channel_id=1, source_target_pairs={{0,32},{32,64},{64,96},{96,128},{128,160},{160,192},{192,224},{224... | collective-permute-start | bytes 15368 | tf_op jit(solution)/shard_map/ppermute | solution.py:24
  21.7 0.1 tile.8
  21.8 1.8 %tile.9 = bf16[4,4,5,3104]{3,1,2,0:T(4,128)(2,1)S(1)} reshape(bf16[4,4,5,32,97]{4,3,1,2,0:T(8,128)(2,1)S(1)} %tile.8) | data formatting | bytes 993280 | tf_op jit(solution)/shard_map/tile | solution.py:72
  23.6 0.2 slice.211
  23.8 0.5 reshape.158
  24.3 0.1 pad.3.clone
  24.4 0.0 collective-permute-done.4
  24.4 0.0 collective-permute-done.5
  24.4 0.0 collective-permute-done.1
  24.5 0.0 collective-permute-done
  24.5 8.4 %collective-permute-start.3 = (bf16[8,32,512]{2,1,0:T(8,128)(2,1)S(1)}, bf16[8,32,512]{2,1,0:T(8,128)(2,1)S(1)}, u32[]{:S(2)}, u32[]{:S(2)}) collective-permute-start(bf16[8,32,512]{2,1,0:T(8,128)(2,1)S(1)} %pad_maximum_fusion.1), channel_id=1, source_target_pairs={{1,0},{2,1},{3,2},{4,3},{5,4},{6,5},{7,6},{8,7},{9,8},{10,9},{11,1... | collective-permute-start | bytes 786440 | tf_op jit(solution)/shard_map/ppermute | solution.py:26
  32.9 1.9 %collective-permute-start.2 = (bf16[8,32,512]{2,1,0:T(8,128)(2,1)S(1)}, bf16[8,32,512]{2,1,0:T(8,128)(2,1)S(1)}, u32[]{:S(2)}, u32[]{:S(2)}) collective-permute-start(bf16[8,32,512]{2,1,0:T(8,128)(2,1)S(1)} %pad_maximum_fusion.1), channel_id=1, source_target_pairs={{0,1},{1,2},{2,3},{3,4},{4,5},{5,6},{6,7},{7,8},{8,9},{9,10},{10,1... | collective-permute-start | bytes 786440 | tf_op jit(solution)/shard_map/ppermute | solution.py:24
  34.9 0.1 rev.3
  35.0 0.1 maximum_maximum_fusion
  35.1 0.1 tile.20
  35.2 1.8 %tile.21 = bf16[4,4,5,3104]{3,1,2,0:T(4,128)(2,1)S(1)} reshape(bf16[4,4,5,32,97]{4,3,1,2,0:T(8,128)(2,1)S(1)} %tile.20) | data formatting | bytes 993280 | tf_op jit(solution)/shard_map/tile | solution.py:72
  37.0 0.2 slice.215
  37.2 0.5 reshape.162
  37.7 0.0 copy-start
  37.7 0.4 collective-permute-done.3
  38.1 7.5 %collective-permute-done.2 = bf16[8,32,512]{2,1,0:T(8,128)(2,1)S(1)} collective-permute-done((bf16[8,32,512]{2,1,0:T(8,128)(2,1)S(1)}, bf16[8,32,512]{2,1,0:T(8,128)(2,1)S(1)}, u32[]{:S(2)}, u32[]{:S(2)}) %collective-permute-start.2) | collective-permute-done | bytes 262176 | tf_op jit(solution)/shard_map/ppermute | solution.py:24
  45.5 0.1 pad_maximum_fusion
  45.7 0.3 convolution_convert_fusion.3
  46.0 0.3 convolution_convert_fusion.2
  46.3 0.3 convolution_convert_fusion.1
  46.6 0.3 convolution_convert_fusion
  47.0 0.4 fusion.1
  47.3 0.2 copy.40
  47.6 0.9 fusion.23
  48.5 0.7 constant_dynamic-update-slice_fusion.11
  49.2 0.9 fusion.22
  50.2 0.7 constant_dynamic-update-slice_fusion.16
  50.8 0.9 fusion.21
  51.8 0.1 fusion.20
  51.9 0.0 copy-start.14
  51.9 0.9 convolution_convert_fusion.4
  52.8 1.3 %fusion.26.part_ref = f32[1024,256]{1,0:T(8,128)} fusion(bf16[128,1024]{1,0:T(8,128)(2,1)S(1)} %bitcast.197, bf16[128,256]{1,0:T(8,128)(2,1)S(1)} %bitcast.221), kind=kOutput, calls=%fused_computation.85 | convolution fusion | flops 67108864 | bytes 1376256 | tf_op jit(solution)/shard_map/dot_general | solution.py:287
  54.1 43.2 %shard_map.85 = bf16[2,16,32,256]{3,2,1,0:T(8,128)(2,1)} custom-call(f32[1024,256]{1,0:T(8,128)} %fusion.26.part_ref), custom_call_target="tpu_custom_call" | custom-call | tf_op jit(solution)/shard_map/pallas_call | solution.py:247
  97.3 2.2 %convert_multiply_fusion = f32[2,16,32,256]{3,2,1,0:T(8,128)} fusion(bf16[2,16,32,256]{3,2,1,0:T(8,128)(2,1)} %shard_map.85), kind=kLoop, calls=%fused_computation.16 | loop fusion | flops 524288 | bytes 1572864 | tf_op jit(solution)/shard_map/mul | solution.py:292
  99.6 0.0 copy-done.2
  99.6 0.9 constant_dynamic-update-slice_fusion.10
  100.7 0.3 convolution_bitcast_fusion.4
  101.0 0.8 copy-done.1
  101.7 0.0 copy-done.11
  101.8 0.0 copy-done.9
  101.8 0.1 copy-done.8
  101.9 0.0 copy-done.7
  102.0 0.3 fusion.4
  102.3 0.5 copy-done.6
  102.8 0.1 copy-done.5
  102.9 0.1 copy-done.4
  103.0 0.1 copy-done.3
  103.1 0.3 fusion.3
  103.6 1.0 fusion.5
  (55 shorter events, 0.6 us)
Async XLA Ops:
  3.7 20.7 %collective-permute-start.4 = (bf16[2,4,5,64]{3,1,2,0:T(4,128)(2,1)S(1)}, bf16[2,4,5,64]{3,1,2,0:T(4,128)(2,1)S(1)}, u32[]{:S(2)}, u32[]{:S(2)}) collective-permute-start(bf16[2,4,5,64]{3,1,2,0:T(4,128)(2,1)S(1)} %get-tuple-element.26), channel_id=1, source_target_pairs={{32,0},{64,32},{96,64},{128,96},{160,128},{192,160},{224,192},{256... | collective-permute-start | bytes 15368 | tf_op jit(solution)/shard_map/ppermute | solution.py:26
  14.1 10.3 %collective-permute-start.1 = (bf16[2,32,512]{2,1,0:T(8,128)(2,1)S(1)}, bf16[2,32,512]{2,1,0:T(8,128)(2,1)S(1)}, u32[]{:S(2)}, u32[]{:S(2)}) collective-permute-start(bf16[2,32,512]{2,1,0:T(8,128)(2,1)S(1)} %get-tuple-element.24), channel_id=1, source_target_pairs={{32,0},{64,32},{96,64},{128,96},{160,128},{192,160},{224,192},{256... | collective-permute-start | bytes 196616 | tf_op jit(solution)/shard_map/ppermute | solution.py:26
  16.1 8.4 %collective-permute-start = (bf16[2,32,512]{2,1,0:T(8,128)(2,1)S(1)}, bf16[2,32,512]{2,1,0:T(8,128)(2,1)S(1)}, u32[]{:S(2)}, u32[]{:S(2)}) collective-permute-start(bf16[2,32,512]{2,1,0:T(8,128)(2,1)S(1)} %get-tuple-element.23), channel_id=1, source_target_pairs={{0,32},{32,64},{64,96},{96,128},{128,160},{160,192},{192,224},{224... | collective-permute-start | bytes 196616 | tf_op jit(solution)/shard_map/ppermute | solution.py:24
  19.7 4.7 %collective-permute-start.5 = (bf16[2,4,5,64]{3,1,2,0:T(4,128)(2,1)S(1)}, bf16[2,4,5,64]{3,1,2,0:T(4,128)(2,1)S(1)}, u32[]{:S(2)}, u32[]{:S(2)}) collective-permute-start(bf16[2,4,5,64]{3,1,2,0:T(4,128)(2,1)S(1)} %get-tuple-element.25), channel_id=1, source_target_pairs={{0,32},{32,64},{64,96},{96,128},{128,160},{160,192},{192,224},{224... | collective-permute-start | bytes 15368 | tf_op jit(solution)/shard_map/ppermute | solution.py:24
  24.5 13.6 %collective-permute-start.3 = (bf16[8,32,512]{2,1,0:T(8,128)(2,1)S(1)}, bf16[8,32,512]{2,1,0:T(8,128)(2,1)S(1)}, u32[]{:S(2)}, u32[]{:S(2)}) collective-permute-start(bf16[8,32,512]{2,1,0:T(8,128)(2,1)S(1)} %pad_maximum_fusion.1), channel_id=1, source_target_pairs={{1,0},{2,1},{3,2},{4,3},{5,4},{6,5},{7,6},{8,7},{9,8},{10,9},{11,1... | collective-permute-start | bytes 786440 | tf_op jit(solution)/shard_map/ppermute | solution.py:26
  32.9 12.6 %collective-permute-start.2 = (bf16[8,32,512]{2,1,0:T(8,128)(2,1)S(1)}, bf16[8,32,512]{2,1,0:T(8,128)(2,1)S(1)}, u32[]{:S(2)}, u32[]{:S(2)}) collective-permute-start(bf16[8,32,512]{2,1,0:T(8,128)(2,1)S(1)} %pad_maximum_fusion.1), channel_id=1, source_target_pairs={{0,1},{1,2},{2,3},{3,4},{4,5},{5,6},{6,7},{7,8},{8,9},{9,10},{10,1... | collective-permute-start | bytes 786440 | tf_op jit(solution)/shard_map/ppermute | solution.py:24
  37.7 7.9 %copy-start = (bf16[4,256,256]{2,1,0:T(8,128)(2,1)S(1)}, bf16[4,256,256]{2,1,0:T(8,128)(2,1)}, u32[]{:S(2)}) copy-start(bf16[4,256,256]{2,1,0:T(8,128)(2,1)} %param.8) | copy-start | bytes 1572868
  51.9 0.9 copy-start.14
  97.3 2.3 %copy-start.2 = (bf16[4,5,96,256]{3,2,1,0:T(8,128)(2,1)S(1)}, bf16[4,5,96,256]{3,2,1,0:T(8,128)(2,1)}, u32[]{:S(2)}) copy-start(bf16[4,5,96,256]{3,2,1,0:T(8,128)(2,1)} %constant_dynamic-update-slice_fusion.11) | copy-start | bytes 2949124
  97.3 3.2 %copy-start.13 = (bf16[384,256]{1,0:T(8,128)(2,1)S(1)}, bf16[384,256]{1,0:T(8,128)(2,1)}, u32[]{:S(2)}) copy-start(bf16[384,256]{1,0:T(8,128)(2,1)} %get-tuple-element.20) | copy-start | bytes 589828
  97.3 3.3 %copy-start.12 = (bf16[384,256]{1,0:T(8,128)(2,1)S(1)}, bf16[384,256]{1,0:T(8,128)(2,1)}, u32[]{:S(2)}) copy-start(bf16[384,256]{1,0:T(8,128)(2,1)} %get-tuple-element.19) | copy-start | bytes 589828
  97.3 3.3 %copy-start.10 = (bf16[384,256]{1,0:T(8,128)(2,1)S(1)}, bf16[384,256]{1,0:T(8,128)(2,1)}, u32[]{:S(2)}) copy-start(bf16[384,256]{1,0:T(8,128)(2,1)} %get-tuple-element.18) | copy-start | bytes 589828
  100.5 1.2 %copy-start.1 = (bf16[4,5,96,256]{3,2,1,0:T(8,128)(2,1)S(1)}, bf16[4,5,96,256]{3,2,1,0:T(8,128)(2,1)}, u32[]{:S(2)}) copy-start(bf16[4,5,96,256]{3,2,1,0:T(8,128)(2,1)} %constant_dynamic-update-slice_fusion.16) | copy-start | bytes 2949124
  100.5 1.2 %copy-start.11 = (bf16[384,256]{1,0:T(8,128)(2,1)S(1)}, bf16[384,256]{1,0:T(8,128)(2,1)}, u32[]{:S(2)}) copy-start(bf16[384,256]{1,0:T(8,128)(2,1)} %get-tuple-element.16) | copy-start | bytes 589828
  100.6 1.2 %copy-start.9 = (bf16[384,256]{1,0:T(8,128)(2,1)S(1)}, bf16[384,256]{1,0:T(8,128)(2,1)}, u32[]{:S(2)}) copy-start(bf16[384,256]{1,0:T(8,128)(2,1)} %get-tuple-element.15) | copy-start | bytes 589828
  100.6 1.3 %copy-start.8 = (bf16[384,256]{1,0:T(8,128)(2,1)S(1)}, bf16[384,256]{1,0:T(8,128)(2,1)}, u32[]{:S(2)}) copy-start(bf16[384,256]{1,0:T(8,128)(2,1)} %get-tuple-element.14) | copy-start | bytes 589828
  100.6 1.3 %copy-start.7 = (bf16[384,256]{1,0:T(8,128)(2,1)S(1)}, bf16[384,256]{1,0:T(8,128)(2,1)}, u32[]{:S(2)}) copy-start(bf16[384,256]{1,0:T(8,128)(2,1)} %get-tuple-element.13) | copy-start | bytes 589828
  101.9 0.9 copy-start.6
  102.0 1.0 copy-start.5
  102.0 1.1 %copy-start.4 = (bf16[384,256]{1,0:T(8,128)(2,1)S(1)}, bf16[384,256]{1,0:T(8,128)(2,1)}, u32[]{:S(2)}) copy-start(bf16[384,256]{1,0:T(8,128)(2,1)} %get-tuple-element.9) | copy-start | bytes 589828
  102.0 1.1 %copy-start.3 = (bf16[384,256]{1,0:T(8,128)(2,1)S(1)}, bf16[384,256]{1,0:T(8,128)(2,1)}, u32[]{:S(2)}) copy-start(bf16[384,256]{1,0:T(8,128)(2,1)} %get-tuple-element.8) | copy-start | bytes 589828

commit v2 on v1

v2 whole, which is shorter than its diff:
```python
import math

import jax
import jax.numpy as jnp
from jax import lax
from jax.experimental import pallas as pl
from jax.experimental.pallas import tpu as pltpu
from jax.sharding import PartitionSpec as P

MESH = pl.DeviceIdType.MESH
PLANE = 16
ZLEN = 16
CHUNK = 32
LATS = 16
LONS = 32
ROWS = 4
REACH = 2
TAPS = 5
WIDE = 32
HALF = 32
BASES = 4
CH = 256
SPAN = ROWS + 2 * REACH
LANES = 128
BF16 = jnp.bfloat16
F32 = jnp.float32


def fill_filters(taps_ref, lat_ref, lon_ref, ft):
    lat_dist = jnp.abs(lax.broadcasted_iota(jnp.int32, (TAPS, 2 * HALF), 0) - REACH)
    lon_dist = jnp.abs(lax.broadcasted_iota(jnp.int32, (TAPS, 2 * HALF), 1) - HALF)
    ft[REACH : REACH + ROWS] = jnp.zeros((ROWS, BASES, 8, LANES), F32)
    for row in range(ROWS):
        ext, count = lat_ref[row], lon_ref[row]
        size = jnp.full((TAPS, 2 * HALF), (2 * ext - 1) * (2 * count - 1), jnp.int32).astype(F32)
        guess = lax.rsqrt(size)
        scale = guess * (1.5 - 0.5 * size * guess * guess)
        scale = jnp.where((lat_dist < ext) & (lon_dist < count), scale, 0.0)
        for basis in range(BASES):
            taps = taps_ref[row, basis].astype(F32) * scale
            ft[REACH + row, basis, 0:TAPS, 0 : 2 * HALF] = taps.astype(BF16).astype(F32)


def slanted(base):
    return pltpu.roll(jnp.broadcast_to(base, (WIDE, LANES)), 0, 1, stride=1, stride_axis=0)


def fill_forward(ft, north, south, bands):
    def one(basis, carry):
        start = pl.multiple_of(basis * WIDE, WIDE)
        for row in range(ROWS):
            for tap in range(TAPS):
                line = row + tap
                base = ft[REACH + row, basis, tap : tap + 1, :]
                if line < REACH:
                    base = base * north
                if line >= REACH + ROWS:
                    base = base * south
                bands[row, pl.ds(start, WIDE), tap * LANES : (tap + 1) * LANES] = slanted(
                    base
                ).astype(BF16)
        return carry

    lax.fori_loop(0, BASES, one, 0)


def convolve(bands, fw, bo):
    for row in range(ROWS):
        patch = fw[row : row + TAPS].reshape(TAPS * LANES, CH)
        sums = jnp.dot(bands[row], patch, preferred_element_type=F32).astype(BF16)
        bo[:, row * WIDE : (row + 1) * WIDE, :] = sums.reshape(BASES, WIDE, CH)


def mix(bo, weight_ref, out_ref):
    total = jnp.dot(bo[0], weight_ref[0], preferred_element_type=F32)
    for basis in range(1, BASES):
        total = total + jnp.dot(bo[basis], weight_ref[basis], preferred_element_type=F32)
    out_ref[...] = total.astype(BF16).reshape(ROWS, WIDE, CH)


def fill_basis_grad(cw, weight_ref, bg):
    cells = cw[...].reshape(SPAN * LANES, CH)

    def one(basis, carry):
        grad = lax.dot_general(
            cells, weight_ref[basis], (((1,), (1,)), ((), ())), preferred_element_type=F32
        )
        start = pl.multiple_of(basis * LANES, LANES)
        bg[:, pl.ds(start, LANES), :] = grad.astype(BF16).reshape(SPAN, LANES, CH)
        return carry

    lax.fori_loop(0, BASES, one, 0)


def fill_reversed(ft, north, south, rt):
    first = lax.broadcasted_iota(jnp.int32, (LANES, LANES), 0)
    second = lax.broadcasted_iota(jnp.int32, (LANES, LANES), 1)
    flip = jnp.where(first + second == 2 * HALF, 1.0, 0.0).astype(BF16)
    flat = ft[...].reshape(SPAN * BASES * 8, LANES).astype(BF16)
    turned = jnp.dot(flat, flip, preferred_element_type=F32)
    rt[...] = turned.reshape(SPAN, BASES, 8, LANES)
    rt[0:REACH] = rt[0:REACH] * north
    rt[REACH + ROWS :] = rt[REACH + ROWS :] * south


def adjoint(rt, bg, wedge, acc, grad_ref):
    acc[...] = jnp.zeros((ROWS * WIDE, CH), F32)
    for line in range(SPAN):
        low, high = max(0, line - TAPS + 1), min(ROWS - 1, line)

        def one(basis, carry):
            start = pl.multiple_of(basis * LANES, LANES)
            for row in range(low, high + 1):
                tap = row + TAPS - 1 - line
                base = rt[line, basis, tap : tap + 1, :]
                wedge[row * WIDE : (row + 1) * WIDE, pl.ds(start, LANES)] = slanted(base).astype(BF16)
            return carry

        lax.fori_loop(0, BASES, one, 0)
        span = slice(low * WIDE, (high + 1) * WIDE)
        acc[span, :] = acc[span, :] + jnp.dot(wedge[span, :], bg[line], preferred_element_type=F32)
    grad_ref[...] = acc[...].astype(BF16).reshape(ROWS, WIDE, CH)


def layer_kernel(
    feat_ref, cot_ref, weight_ref, taps_ref, lat_ref, lon_ref,
    out_ref, grad_ref, sum_ref,
    fw, cw, ft, rt, bands, bo, bg, wedge, acc, part, pair_out, pair_in, half, plane_in, zbuf,
    feat_send, feat_recv, cot_send, cot_recv, ft_send, ft_recv, pair_send, pair_recv,
    plane_send, plane_recv, z_send, z_recv, all_send, all_recv, near_send, near_recv,
):
    lat = lax.axis_index("lat")
    lon = lax.axis_index("lon")
    core = lat % 2
    y_lo = (lat // 2) % 2
    x = lat // 4
    z = lon % ZLEN
    y_hi = lon // ZLEN
    spot = x * 4 + y_hi * 2 + y_lo
    partner = (lat + 1 - 2 * core, lon)

    def plane_device(index):
        return ((index // 4) * 4 + (index % 2) * 2 + core, ((index // 2) % 2) * ZLEN + z)

    def z_device(index):
        return (lat, y_hi * ZLEN + index)

    def beside(up, right):
        return ((lat + LATS + up) % LATS, (lon + LONS + right) % LONS)

    ways = [(0, 1), (0, -1), (1, 1), (1, -1), (-1, 1), (-1, -1), (1, 0), (-1, 0)]

    def remote(src, dst, send, recv, device):
        return pltpu.make_async_remote_copy(
            src_ref=src, dst_ref=dst, send_sem=send, recv_sem=recv,
            device_id=device, device_id_type=MESH,
        )

    barrier = pltpu.get_barrier_semaphore()
    for way in ways:
        pl.semaphore_signal(barrier, inc=1, device_id=beside(*way), device_id_type=MESH)

    def greet(step, carry):
        pl.semaphore_signal(
            barrier, inc=1, device_id=z_device((z + step) % ZLEN), device_id_type=MESH
        )
        pl.semaphore_signal(
            barrier, inc=1, device_id=plane_device((spot + step) % PLANE), device_id_type=MESH
        )
        return carry

    lax.fori_loop(1, PLANE, greet, 0)

    north = jnp.where(lat > 0, 1.0, 0.0)
    south = jnp.where(lat < LATS - 1, 1.0, 0.0)
    inner = slice(REACH, REACH + ROWS)
    blank = jnp.zeros((SPAN, LANES - 3 * WIDE, CH), BF16)
    fw[:, 3 * WIDE :, :] = blank
    cw[:, 3 * WIDE :, :] = blank
    fw[inner, WIDE : 2 * WIDE, :] = feat_ref[...]
    cw[inner, WIDE : 2 * WIDE, :] = cot_ref[...]
    fill_filters(taps_ref, lat_ref, lon_ref, ft)
    fill_forward(ft, north, south, bands)
    pl.semaphore_wait(barrier, len(ways) + (PLANE - 1) + (ZLEN - 1))

    def halo(source, window, send, recv):
        copies = []
        for index, (up, right) in enumerate(ways):
            own = slice(0, ROWS) if up == 0 else slice(ROWS - REACH, ROWS) if up > 0 else slice(0, REACH)
            line = inner if up == 0 else slice(0, REACH) if up > 0 else slice(REACH + ROWS, SPAN)
            left = WIDE * (1 - right)
            copies.append(
                remote(
                    source.at[own], window.at[line, left : left + WIDE],
                    send.at[index], recv.at[index], beside(up, right),
                )
            )
        return copies

    feat_copies = halo(feat_ref, fw, feat_send, feat_recv)
    cot_copies = halo(cot_ref, cw, cot_send, cot_recv)
    ft_copies = [
        remote(ft.at[ROWS : ROWS + REACH], ft.at[0:REACH], ft_send.at[0], ft_recv.at[0], beside(1, 0)),
        remote(ft.at[REACH : 2 * REACH], ft.at[REACH + ROWS :], ft_send.at[1], ft_recv.at[1], beside(-1, 0)),
    ]
    for copy in feat_copies + ft_copies + cot_copies:
        copy.start()
    for copy in feat_copies:
        copy.wait_recv()
    convolve(bands, fw, bo)

    cells = cot_ref[...].reshape(ROWS * WIDE, CH)

    def share(basis):
        return lax.dot_general(bo[basis], cells, (((0,), (0,)), ((), ())), preferred_element_type=F32)

    def pair_copy(index):
        span = pl.ds(pl.multiple_of(index * CH, CH), CH)
        return remote(pair_out.at[span], pair_in.at[span], pair_send.at[index], pair_recv.at[index], partner)

    for index in range(2):
        pair_out[index * CH : (index + 1) * CH, :] = share((1 - core) * 2 + index).astype(BF16)
        pair_copy(index).start()
    for index in range(2):
        part[index * CH : (index + 1) * CH, :] = share(core * 2 + index)
    per = PLANE // 2
    for index in range(2):
        pair_copy(index).wait_recv()
        span = slice(index * CH, (index + 1) * CH)
        total = part[span, :] + pair_in[span, :].astype(F32)
        half[index * per : (index + 1) * per] = total.astype(BF16).reshape(per, CHUNK, CH)

    def plane_copy(step):
        target = (spot + step) % PLANE
        return remote(
            half.at[target], plane_in.at[step], plane_send.at[step], plane_recv.at[step],
            plane_device(target),
        )

    def plane_start(step, carry):
        plane_copy(step).start()
        return carry

    def plane_add(step, carry):
        plane_copy(step).wait_recv()
        return carry + plane_in[step].astype(F32)

    lax.fori_loop(1, PLANE, plane_start, 0)
    mix(bo, weight_ref, out_ref)
    for copy in cot_copies + ft_copies:
        copy.wait_recv()
    fill_basis_grad(cw, weight_ref, bg)
    chunk = lax.fori_loop(1, PLANE, plane_add, half[spot].astype(F32))
    zbuf[z] = chunk.astype(BF16)

    def z_copy(step):
        return remote(
            zbuf.at[z], zbuf.at[z], z_send.at[step], z_recv.at[z], z_device((z + step) % ZLEN)
        )

    def z_start(step, carry):
        z_copy(step).start()
        return carry

    def z_wait(step, carry):
        source = (z + step) % ZLEN
        remote(
            zbuf.at[source], zbuf.at[source], z_send.at[step], z_recv.at[source], z_device(source)
        ).wait_recv()
        return carry

    lax.fori_loop(1, ZLEN, z_start, 0)
    fill_reversed(ft, north, south, rt)
    adjoint(rt, bg, wedge, acc, grad_ref)
    lax.fori_loop(1, ZLEN, z_wait, 0)
    chunk = zbuf[0].astype(F32)
    for source in range(1, ZLEN):
        chunk = chunk + zbuf[source].astype(F32)
    sum_ref[core, spot] = chunk.astype(BF16)

    def all_copy(step):
        return remote(
            sum_ref.at[core, spot], sum_ref.at[core, spot], all_send.at[step], all_recv.at[spot],
            plane_device((spot + step) % PLANE),
        )

    def near_copy(index):
        return remote(
            sum_ref.at[core, index], sum_ref.at[core, index], near_send.at[index],
            near_recv.at[index], partner,
        )

    def all_start(step, carry):
        all_copy(step).start()
        return carry

    def all_forward(step, carry):
        source = (spot + step) % PLANE
        remote(
            sum_ref.at[core, source], sum_ref.at[core, source], all_send.at[step],
            all_recv.at[source], plane_device(source),
        ).wait_recv()
        near_copy(source).start()
        return carry

    lax.fori_loop(1, PLANE, all_start, 0)
    near_copy(spot).start()
    for copy in feat_copies + cot_copies + ft_copies:
        copy.wait_send()
    for index in range(2):
        pair_copy(index).wait_send()
    lax.fori_loop(1, PLANE, all_forward, 0)

    def finish(step, carry):
        plane_copy(step).wait_send()
        z_copy(step).wait_send()
        all_copy(step).wait_send()
        return carry

    lax.fori_loop(1, PLANE, finish, 0)

    def near_finish(index, carry):
        near_copy(index).wait_send()
        remote(
            sum_ref.at[1 - core, index], sum_ref.at[1 - core, index], near_send.at[index],
            near_recv.at[index], partner,
        ).wait_recv()
        return carry

    lax.fori_loop(0, PLANE, near_finish, 0)


def layer(features, cotangent, weight, filter_taps, lat_ext, lon_count):
    dma = pltpu.SemaphoreType.DMA
    vmem = pl.BlockSpec(memory_space=pltpu.VMEM)
    smem = pl.BlockSpec(memory_space=pltpu.SMEM)
    return pl.pallas_call(
        layer_kernel,
        out_shape=[
            jax.ShapeDtypeStruct((ROWS, WIDE, CH), BF16),
            jax.ShapeDtypeStruct((ROWS, WIDE, CH), BF16),
            jax.ShapeDtypeStruct((2, PLANE, CHUNK, CH), BF16),
        ],
        in_specs=[vmem, vmem, vmem, vmem, smem, smem],
        out_specs=[vmem, vmem, vmem],
        scratch_shapes=[
            pltpu.VMEM((SPAN, LANES, CH), BF16),
            pltpu.VMEM((SPAN, LANES, CH), BF16),
            pltpu.VMEM((SPAN, BASES, 8, LANES), F32),
            pltpu.VMEM((SPAN, BASES, 8, LANES), F32),
            pltpu.VMEM((ROWS, BASES * WIDE, TAPS * LANES), BF16),
            pltpu.VMEM((BASES, ROWS * WIDE, CH), BF16),
            pltpu.VMEM((SPAN, BASES * LANES, CH), BF16),
            pltpu.VMEM((ROWS * WIDE, BASES * LANES), BF16),
            pltpu.VMEM((ROWS * WIDE, CH), F32),
            pltpu.VMEM((2 * CH, CH), F32),
            pltpu.VMEM((2 * CH, CH), BF16),
            pltpu.VMEM((2 * CH, CH), BF16),
            pltpu.VMEM((PLANE, CHUNK, CH), BF16),
            pltpu.VMEM((PLANE, CHUNK, CH), BF16),
            pltpu.VMEM((ZLEN, CHUNK, CH), BF16),
            dma((8,)), dma((8,)), dma((8,)), dma((8,)), dma((2,)), dma((2,)), dma((2,)), dma((2,)),
            dma((PLANE,)), dma((PLANE,)), dma((ZLEN,)), dma((ZLEN,)),
            dma((PLANE,)), dma((PLANE,)), dma((PLANE,)), dma((PLANE,)),
        ],
        compiler_params=pltpu.CompilerParams(collective_id=0, has_side_effects=True),
    )(features, cotangent, weight, filter_taps, lat_ext, lon_count)


def per_device(features, cotangent, weight, filter_taps, lat_ext, lon_count):
    output, field_grad, total = layer(features, cotangent, weight, filter_taps, lat_ext, lon_count)
    cells = LATS * ROWS * LONS * WIDE
    weight_grad = (total.astype(F32) * (1.0 / math.sqrt(cells))).reshape(BASES, CH, CH)
    return (output, field_grad, weight_grad)


def solution(mesh):
    in_specs = (
        P("lat", "lon", None),
        P("lat", "lon", None),
        P(),
        P("lat", None, None, None),
        P("lat"),
        P("lat"),
    )
    out_specs = (P("lat", "lon", None), P("lat", "lon", None), P())
    return jax.shard_map(
        per_device, mesh=mesh, in_specs=in_specs, out_specs=out_specs, check_vma=False
    )
```

time: 105 us -> 62.2 us (0.59)
  starting transfers between devices: 26.6 us -> 0 us
  Pallas kernels: 43.2 us -> 56.3 us
  local copies, waits for them, and re-layouts: 14.7 us -> 2.85 us
  waiting for transfers between devices: 7.82 us -> 0 us
  matrix products: 5.58 us -> 0 us
  other arithmetic: 5.49 us -> 2.15 us
    ppermute x6 -> x0, starting transfers between devices: 26.6 us -> none  [the longest x3 19.1 us: extended(): lax.ppermute(head, axis, [((i + 1) % count, i) for i in range(ends)])]
    pallas_call x1, Pallas kernels: 43.2 us -> 56.3 us  [layer(): pl.pallas_call(layer_kernel, out_shape=[jax.ShapeDtypeStruct((ROWS, WIDE,...]
    ppermute x6 -> x0, waiting for transfers between devices: 7.82 us -> none  [the longest x3 7.46 us: extended(): lax.ppermute(tail, axis, [(i, (i + 1) % count) for i in range(ends)])]
    dot_general x11 -> x0, matrix products: 5.58 us -> none  [the longest x4 1.88 us: gather_adjoint(): jnp.einsum('oejn,oenc->ojc', banded[:, basis_index], patches, preferred_e...]
    another operation x9 -> x0, local copies, waits for them, and re-layouts: 3.88 us -> none  [the longest x4 3.81 us: band_matrix(): repeated = jnp.tile(padded, (1,) * len(leading) + (lon_width,))]
    slice x9 -> x0, local copies, waits for them, and re-layouts: 3.27 us -> none  [the longest x4 2.88 us: gather_adjoint(): grad_window[last - offset:last - offset + row_count]]
    unnamed x53 -> x7, local copies, waits for them, and re-layouts: 5.22 us -> 2.85 us
    lt x2 -> x0, other arithmetic: 1.46 us -> none  [the longest x1 0.73 us: make_filters(): lon_dist[None, None, :] < lon_count[:, None, None]]
  transfers between devices with their start and end apart: 6 -> 0, of which waited for: 2 -> 0; matrix products, arithmetic and copies ran while one was open for 7% -> 0% of each run, Pallas kernels for 0% -> 0%
where the time goes in v2:
time: 62.2 us; the launch traced here: 61.9 us
  Pallas kernels  56.3 us (91%)
  local copies, waits for them, and re-layouts  2.85 us (5%)
  other arithmetic  2.15 us (3%)
  between operations  0.65 us (1%)
    pallas_call x1, Pallas kernels, layer(): pl.pallas_call(layer_kernel, out_shape=[jax.ShapeDtypeStruct((ROWS, WIDE,...  56.3 us
    unnamed x7, local copies, waits for them, and re-layouts  2.85 us
    mul x1, other arithmetic, per_device(): total.astype(F32) * (1.0 / math.sqrt(cells))  2.15 us

profile of v2, /device:TPU:1, one launch (start us, length us, event | category | flops | bytes accessed | tf_op | source)
XLA Modules:
  0.0 61.9 jit_solution(9154996537556281960)
XLA Ops:
  0.6 1.4 %copy.9.taps_ref = bf16[4,4,5,64]{3,2,1,0:T(8,128)(2,1)} copy(bf16[4,4,5,64]{3,1,2,0:T(4,128)(2,1)} %param.9) | data formatting | bytes 20480 | tf_op args[3]
  2.0 56.3 %shard_map.85 = (bf16[4,32,256]{2,1,0:T(8,128)(2,1)}, bf16[4,32,256]{2,1,0:T(8,128)(2,1)}, bf16[2,16,32,256]{3,2,1,0:T(8,128)(2,1)}) custom-call(bf16[4,32,256]{2,1,0:T(8,128)(2,1)} %feat_ref.1, bf16[4,32,256]{2,1,0:T(8,128)(2,1)} %cot_ref.1, bf16[4,256,256]{2,1,0:T(8,128)(2,1)} %weight_ref.1, bf16[4,4,5,64]{3,2,1,0:T(8,128)(2,1)} %copy.9.taps_ref, ...), custom_call_target="tpu_custom_call" | custom-call | tf_op jit(solution)/shard_map/pallas_call | solution.py:337
  58.3 0.0 copy-start.1
  58.3 2.1 %convert_multiply_fusion = f32[2,16,32,256]{3,2,1,0:T(8,128)} fusion(bf16[2,16,32,256]{3,2,1,0:T(8,128)(2,1)} %get-tuple-element.8), kind=kLoop, calls=%fused_computation | loop fusion | flops 524288 | bytes 1572864 | tf_op jit(solution)/shard_map/mul | solution.py:373
  60.4 0.0 copy-done.1
  60.4 0.0 copy-start
  60.4 0.6 %copy.12 = bf16[4,32,256]{2,1,0:T(8,128)(2,1)} copy(bf16[4,32,256]{2,1,0:T(8,128)(2,1)S(1)} %copy-done.1) | data formatting | bytes 131072
  61.1 0.2 copy-done
  61.3 0.6 %copy.13 = bf16[4,32,256]{2,1,0:T(8,128)(2,1)} copy(bf16[4,32,256]{2,1,0:T(8,128)(2,1)S(1)} %copy-done) | data formatting | bytes 131072
Async XLA Ops:
  58.3 2.2 %copy-start.1 = (bf16[4,32,256]{2,1,0:T(8,128)(2,1)S(1)}, bf16[4,32,256]{2,1,0:T(8,128)(2,1)}, u32[]{:S(2)}) copy-start(bf16[4,32,256]{2,1,0:T(8,128)(2,1)} %get-tuple-element.12) | copy-start | bytes 196612
  60.4 0.9 %copy-start = (bf16[4,32,256]{2,1,0:T(8,128)(2,1)S(1)}, bf16[4,32,256]{2,1,0:T(8,128)(2,1)}, u32[]{:S(2)}) copy-start(bf16[4,32,256]{2,1,0:T(8,128)(2,1)} %get-tuple-element.13) | copy-start | bytes 196612

commit v3 on v2

v3 whole, which is shorter than its diff:
```python
import math

import jax
import jax.numpy as jnp
from jax import lax
from jax.experimental import pallas as pl
from jax.experimental.pallas import tpu as pltpu
from jax.sharding import PartitionSpec as P

MESH = pl.DeviceIdType.MESH
GROUP = 32
ZLEN = 16
ZFAR = 8
CHUNK = 16
LATS = 16
LONS = 32
ROWS = 4
REACH = 2
TAPS = 5
WIDE = 32
HALF = 32
BASES = 4
CH = 256
SPAN = ROWS + 2 * REACH
LANES = 128
BF16 = jnp.bfloat16
F32 = jnp.float32


def fill_filters(taps_ref, lat_ref, lon_ref, ft):
    lon_dist = jnp.abs(lax.broadcasted_iota(jnp.int32, (BASES, 2 * HALF), 1) - HALF)
    ft[REACH : REACH + ROWS] = jnp.zeros((ROWS, TAPS, 8, LANES), F32)
    for row in range(ROWS):
        ext, count = lat_ref[row], lon_ref[row]
        size = jnp.full((BASES, 2 * HALF), (2 * ext - 1) * (2 * count - 1), jnp.int32).astype(F32)
        guess = lax.rsqrt(size)
        scale = guess * (1.5 - 0.5 * size * guess * guess)
        scale = jnp.where(lon_dist < count, scale, 0.0)
        for tap in range(TAPS):
            held = jnp.where(abs(tap - REACH) < ext, scale, 0.0)
            taps = taps_ref[row, tap].astype(F32) * held
            ft[REACH + row, tap, 0:BASES, 0 : 2 * HALF] = taps.astype(BF16).astype(F32)


def slanted(base):
    return pltpu.roll(jnp.broadcast_to(base, (WIDE, LANES)), 0, 1, stride=1, stride_axis=0)


def fill_forward(ft, north, south, bands):
    def one(basis, carry):
        start = pl.multiple_of(basis * WIDE, WIDE)
        for row in range(ROWS):
            for tap in range(TAPS):
                line = row + tap
                base = ft[REACH + row, tap, pl.ds(basis, 1), :]
                if line < REACH:
                    base = base * north
                if line >= REACH + ROWS:
                    base = base * south
                bands[row, pl.ds(start, WIDE), tap * LANES : (tap + 1) * LANES] = slanted(
                    base
                ).astype(BF16)
        return carry

    lax.fori_loop(0, BASES, one, 0)


def convolve(bands, fw, bo):
    for row in range(ROWS):
        patch = fw[row : row + TAPS].reshape(TAPS * LANES, CH)
        sums = jnp.dot(bands[row], patch, preferred_element_type=F32).astype(BF16)
        bo[:, row * WIDE : (row + 1) * WIDE, :] = sums.reshape(BASES, WIDE, CH)


def mix(bo, weight_ref, out_ref):
    total = jnp.dot(bo[0], weight_ref[0], preferred_element_type=F32)
    for basis in range(1, BASES):
        total = total + jnp.dot(bo[basis], weight_ref[basis], preferred_element_type=F32)
    out_ref[...] = total.astype(BF16).reshape(ROWS, WIDE, CH)


def fill_basis_grad(cw, weight_ref, bg):
    cells = cw[...].reshape(SPAN * LANES, CH)

    def one(basis, carry):
        grad = lax.dot_general(
            cells, weight_ref[basis], (((1,), (1,)), ((), ())), preferred_element_type=F32
        )
        start = pl.multiple_of(basis * LANES, LANES)
        bg[:, pl.ds(start, LANES), :] = grad.astype(BF16).reshape(SPAN, LANES, CH)
        return carry

    lax.fori_loop(0, BASES, one, 0)


def fill_reversed(ft, north, south, rt):
    first = lax.broadcasted_iota(jnp.int32, (LANES, LANES), 0)
    second = lax.broadcasted_iota(jnp.int32, (LANES, LANES), 1)
    flip = jnp.where(first + second == 2 * HALF, 1.0, 0.0).astype(BF16)
    flat = ft[...].reshape(SPAN * TAPS * 8, LANES).astype(BF16)
    turned = jnp.dot(flat, flip, preferred_element_type=F32)
    rt[...] = turned.reshape(SPAN, TAPS, 8, LANES)
    rt[0:REACH] = rt[0:REACH] * north
    rt[REACH + ROWS :] = rt[REACH + ROWS :] * south


def adjoint(rt, bg, wedge, acc, grad_ref):
    acc[...] = jnp.zeros((ROWS * WIDE, CH), F32)
    for line in range(SPAN):
        low, high = max(0, line - TAPS + 1), min(ROWS - 1, line)

        def one(basis, carry):
            start = pl.multiple_of(basis * LANES, LANES)
            for row in range(low, high + 1):
                tap = row + TAPS - 1 - line
                base = rt[line, tap, pl.ds(basis, 1), :]
                wedge[row * WIDE : (row + 1) * WIDE, pl.ds(start, LANES)] = slanted(base).astype(BF16)
            return carry

        lax.fori_loop(0, BASES, one, 0)
        span = slice(low * WIDE, (high + 1) * WIDE)
        acc[span, :] = acc[span, :] + jnp.dot(wedge[span, :], bg[line], preferred_element_type=F32)
    grad_ref[...] = acc[...].astype(BF16).reshape(ROWS, WIDE, CH)


def layer_kernel(
    feat_any, cot_any, weight_any, taps_ref, lat_ref, lon_ref,
    out_ref, grad_ref, sum_ref,
    fw, cw, weight_ref, ft, rt, bands, bo, bg, wedge, acc, part, pair_out, pair_in, half, group_in, zbuf,
    own_sem, feat_send, feat_recv, cot_send, cot_recv, ft_send, ft_recv, pair_send, pair_recv,
    group_send, group_recv, z_send, z_recv, all_send, all_recv, near_send, near_recv,
    hop_sem, leap_sem,
):
    lat = lax.axis_index("lat")
    lon = lax.axis_index("lon")
    core = lat % 2
    y_lo = (lat // 2) % 2
    x = lat // 4
    z = lon % ZLEN
    z_lo = z % 2
    z_hi = z // 2
    y_hi = lon // ZLEN
    spot = (x * 4 + y_hi * 2 + y_lo) * 2 + z_lo
    partner = (lat + 1 - 2 * core, lon)

    def group_device(index):
        place = index // 2
        return (
            (place // 4) * 4 + (place % 2) * 2 + core,
            ((place // 2) % 2) * ZLEN + z_hi * 2 + index % 2,
        )

    def z_device(index):
        return (lat, y_hi * ZLEN + index)

    def far_device(index):
        return z_device(index * 2 + z_lo)

    def beside(up, right):
        return ((lat + LATS + up) % LATS, (lon + LONS + right) % LONS)

    ways = [(0, 1), (0, -1), (1, 1), (1, -1), (-1, 1), (-1, -1), (1, 0), (-1, 0)]

    def remote(src, dst, send, recv, device):
        return pltpu.make_async_remote_copy(
            src_ref=src, dst_ref=dst, send_sem=send, recv_sem=recv,
            device_id=device, device_id_type=MESH,
        )

    barrier = pltpu.get_barrier_semaphore()
    for way in ways:
        pl.semaphore_signal(barrier, inc=1, device_id=beside(*way), device_id_type=MESH)
    pl.semaphore_signal(barrier, inc=1, device_id=z_device((z + 2) % ZLEN), device_id_type=MESH)
    pl.semaphore_signal(
        barrier, inc=1, device_id=z_device((z + ZLEN - 2) % ZLEN), device_id_type=MESH
    )

    def greet(step, carry):
        pl.semaphore_signal(
            barrier, inc=1, device_id=group_device((spot + step) % GROUP), device_id_type=MESH
        )
        return carry

    lax.fori_loop(1, GROUP, greet, 0)

    north = jnp.where(lat > 0, 1.0, 0.0)
    south = jnp.where(lat < LATS - 1, 1.0, 0.0)
    inner = slice(REACH, REACH + ROWS)
    middle = slice(WIDE, 2 * WIDE)
    own_copies = [
        pltpu.make_async_copy(feat_any, fw.at[inner, middle], own_sem.at[0]),
        pltpu.make_async_copy(cot_any, cw.at[inner, middle], own_sem.at[1]),
        pltpu.make_async_copy(weight_any, weight_ref, own_sem.at[2]),
    ]
    for copy in own_copies:
        copy.start()
    blank = jnp.zeros((SPAN, LANES - 3 * WIDE, CH), BF16)
    fw[:, 3 * WIDE :, :] = blank
    cw[:, 3 * WIDE :, :] = blank
    fill_filters(taps_ref, lat_ref, lon_ref, ft)
    fill_forward(ft, north, south, bands)
    own_copies[0].wait()
    own_copies[1].wait()
    pl.semaphore_wait(barrier, len(ways) + 2 + (GROUP - 1))

    def halo(window, send, recv):
        copies = []
        for index, (up, right) in enumerate(ways):
            own = inner if up == 0 else slice(ROWS, ROWS + REACH) if up > 0 else slice(REACH, 2 * REACH)
            line = inner if up == 0 else slice(0, REACH) if up > 0 else slice(REACH + ROWS, SPAN)
            left = WIDE * (1 - right)
            copies.append(
                remote(
                    window.at[own, middle], window.at[line, left : left + WIDE],
                    send.at[index], recv.at[index], beside(up, right),
                )
            )
        return copies

    feat_copies = halo(fw, feat_send, feat_recv)
    cot_copies = halo(cw, cot_send, cot_recv)
    ft_copies = [
        remote(ft.at[ROWS : ROWS + REACH], ft.at[0:REACH], ft_send.at[0], ft_recv.at[0], beside(1, 0)),
        remote(ft.at[REACH : 2 * REACH], ft.at[REACH + ROWS :], ft_send.at[1], ft_recv.at[1], beside(-1, 0)),
    ]
    for copy in feat_copies:
        copy.start()
    pl.semaphore_signal(hop_sem, inc=1, device_id=z_device((z + 2) % ZLEN), device_id_type=MESH)
    pl.semaphore_signal(hop_sem, inc=1, device_id=z_device((z + ZLEN - 2) % ZLEN), device_id_type=MESH)
    for copy in feat_copies:
        copy.wait_recv()
    for copy in cot_copies + ft_copies:
        copy.start()
    pl.semaphore_wait(hop_sem, 2)
    pl.semaphore_signal(leap_sem, inc=1, device_id=z_device((z + 4) % ZLEN), device_id_type=MESH)
    pl.semaphore_signal(leap_sem, inc=1, device_id=z_device((z + ZLEN - 4) % ZLEN), device_id_type=MESH)
    convolve(bands, fw, bo)

    cells = cw[inner, middle, :].reshape(ROWS * WIDE, CH)

    def share(basis):
        return lax.dot_general(bo[basis], cells, (((0,), (0,)), ((), ())), preferred_element_type=F32)

    def pair_copy(index):
        span = pl.ds(pl.multiple_of(index * CH, CH), CH)
        return remote(pair_out.at[span], pair_in.at[span], pair_send.at[index], pair_recv.at[index], partner)

    for index in range(2):
        pair_out[index * CH : (index + 1) * CH, :] = share((1 - core) * 2 + index).astype(BF16)
        pair_copy(index).start()
    for index in range(2):
        part[index * CH : (index + 1) * CH, :] = share(core * 2 + index)
    per = GROUP // 2
    for index in range(2):
        pair_copy(index).wait_recv()
        span = slice(index * CH, (index + 1) * CH)
        total = part[span, :] + pair_in[span, :].astype(F32)
        half[index * per : (index + 1) * per] = total.astype(BF16).reshape(per, CHUNK, CH)

    def group_copy(step):
        target = (spot + step) % GROUP
        return remote(
            half.at[target], group_in.at[step], group_send.at[step], group_recv.at[step],
            group_device(target),
        )

    def group_start(step, carry):
        group_copy(step).start()
        return carry

    def group_add(step, carry):
        group_copy(step).wait_recv()
        return carry + group_in[step].astype(F32)

    lax.fori_loop(1, GROUP, group_start, 0)
    own_copies[2].wait()
    mix(bo, weight_ref, out_ref)
    for copy in cot_copies + ft_copies:
        copy.wait_recv()
    fill_basis_grad(cw, weight_ref, bg)
    chunk = lax.fori_loop(1, GROUP, group_add, half[spot].astype(F32))
    zbuf[z_hi] = chunk.astype(BF16)
    pl.semaphore_wait(leap_sem, 2)

    def z_copy(step):
        return remote(
            zbuf.at[z_hi], zbuf.at[z_hi], z_send.at[step], z_recv.at[z_hi],
            far_device((z_hi + step) % ZFAR),
        )

    def z_start(step, carry):
        z_copy(step).start()
        return carry

    def z_wait(step, carry):
        source = (z_hi + step) % ZFAR
        remote(
            zbuf.at[source], zbuf.at[source], z_send.at[step], z_recv.at[source], far_device(source)
        ).wait_recv()
        return carry

    lax.fori_loop(1, ZFAR, z_start, 0)
    fill_reversed(ft, north, south, rt)
    adjoint(rt, bg, wedge, acc, grad_ref)
    lax.fori_loop(1, ZFAR, z_wait, 0)
    chunk = zbuf[0].astype(F32)
    for source in range(1, ZFAR):
        chunk = chunk + zbuf[source].astype(F32)
    sum_ref[core, spot] = chunk.astype(BF16)

    def all_copy(step):
        return remote(
            sum_ref.at[core, spot], sum_ref.at[core, spot], all_send.at[step], all_recv.at[spot],
            group_device((spot + step) % GROUP),
        )

    def near_copy(index):
        return remote(
            sum_ref.at[core, index], sum_ref.at[core, index], near_send.at[index],
            near_recv.at[index], partner,
        )

    def all_start(step, carry):
        all_copy(step).start()
        return carry

    def all_forward(step, carry):
        source = (spot + step) % GROUP
        remote(
            sum_ref.at[core, source], sum_ref.at[core, source], all_send.at[step],
            all_recv.at[source], group_device(source),
        ).wait_recv()
        near_copy(source).start()
        return carry

    lax.fori_loop(1, GROUP, all_start, 0)
    near_copy(spot).start()
    for copy in feat_copies + cot_copies + ft_copies:
        copy.wait_send()
    for index in range(2):
        pair_copy(index).wait_send()

    def z_finish(step, carry):
        z_copy(step).wait_send()
        return carry

    lax.fori_loop(1, ZFAR, z_finish, 0)
    lax.fori_loop(1, GROUP, all_forward, 0)

    def finish(step, carry):
        group_copy(step).wait_send()
        all_copy(step).wait_send()
        return carry

    lax.fori_loop(1, GROUP, finish, 0)

    def near_finish(index, carry):
        near_copy(index).wait_send()
        remote(
            sum_ref.at[1 - core, index], sum_ref.at[1 - core, index], near_send.at[index],
            near_recv.at[index], partner,
        ).wait_recv()
        return carry

    lax.fori_loop(0, GROUP, near_finish, 0)


def layer(features, cotangent, weight, filter_taps, lat_ext, lon_count):
    dma = pltpu.SemaphoreType.DMA
    vmem = pl.BlockSpec(memory_space=pltpu.VMEM)
    smem = pl.BlockSpec(memory_space=pltpu.SMEM)
    anywhere = pl.BlockSpec(memory_space=pl.ANY)
    return pl.pallas_call(
        layer_kernel,
        out_shape=[
            pltpu.VMEM((ROWS, WIDE, CH), BF16),
            pltpu.VMEM((ROWS, WIDE, CH), BF16),
            pltpu.VMEM((2, GROUP, CHUNK, CH), BF16),
        ],
        in_specs=[anywhere, anywhere, anywhere, vmem, smem, smem],
        out_specs=[vmem, vmem, vmem],
        scratch_shapes=[
            pltpu.VMEM((SPAN, LANES, CH), BF16),
            pltpu.VMEM((SPAN, LANES, CH), BF16),
            pltpu.VMEM((BASES, CH, CH), BF16),
            pltpu.VMEM((SPAN, TAPS, 8, LANES), F32),
            pltpu.VMEM((SPAN, TAPS, 8, LANES), F32),
            pltpu.VMEM((ROWS, BASES * WIDE, TAPS * LANES), BF16),
            pltpu.VMEM((BASES, ROWS * WIDE, CH), BF16),
            pltpu.VMEM((SPAN, BASES * LANES, CH), BF16),
            pltpu.VMEM((ROWS * WIDE, BASES * LANES), BF16),
            pltpu.VMEM((ROWS * WIDE, CH), F32),
            pltpu.VMEM((2 * CH, CH), F32),
            pltpu.VMEM((2 * CH, CH), BF16),
            pltpu.VMEM((2 * CH, CH), BF16),
            pltpu.VMEM((GROUP, CHUNK, CH), BF16),
            pltpu.VMEM((GROUP, CHUNK, CH), BF16),
            pltpu.VMEM((ZFAR, CHUNK, CH), BF16),
            dma((3,)),
            dma((8,)), dma((8,)), dma((8,)), dma((8,)), dma((2,)), dma((2,)), dma((2,)), dma((2,)),
            dma((GROUP,)), dma((GROUP,)), dma((ZFAR,)), dma((ZFAR,)),
            dma((GROUP,)), dma((GROUP,)), dma((GROUP,)), dma((GROUP,)),
            pltpu.SemaphoreType.REGULAR, pltpu.SemaphoreType.REGULAR,
        ],
        compiler_params=pltpu.CompilerParams(collective_id=0, has_side_effects=True),
    )(features, cotangent, weight, filter_taps, lat_ext, lon_count)


PIECES = 8


def write_kernel(scale, out_ref, grad_ref, sum_ref, out_any, grad_any, total_any, wide, sem):
    copies = [
        pltpu.make_async_copy(out_ref, out_any, sem.at[PIECES]),
        pltpu.make_async_copy(grad_ref, grad_any, sem.at[PIECES + 1]),
    ]
    for copy in copies:
        copy.start()
    per = 2 * GROUP // PIECES
    for index in range(PIECES):
        side, first = (index * per) // GROUP, (index * per) % GROUP
        wide[side, first : first + per] = sum_ref[side, first : first + per].astype(F32) * scale
        copy = pltpu.make_async_copy(
            wide.at[side, first : first + per], total_any.at[side, first : first + per], sem.at[index]
        )
        copy.start()
        copies.append(copy)
    for copy in copies:
        copy.wait()


def write(scale, output, grad, total):
    vmem = pl.BlockSpec(memory_space=pltpu.VMEM)
    anywhere = pl.BlockSpec(memory_space=pl.ANY)
    return pl.pallas_call(
        lambda *refs: write_kernel(scale, *refs),
        out_shape=[
            jax.ShapeDtypeStruct(output.shape, BF16),
            jax.ShapeDtypeStruct(grad.shape, BF16),
            jax.ShapeDtypeStruct(total.shape, F32),
        ],
        in_specs=[vmem, vmem, vmem],
        out_specs=[anywhere, anywhere, anywhere],
        scratch_shapes=[pltpu.VMEM(total.shape, F32), pltpu.SemaphoreType.DMA((PIECES + 2,))],
        name="write",
    )(*(pltpu.with_memory_space_constraint(held, pltpu.VMEM) for held in (output, grad, total)))


def per_device(features, cotangent, weight, filter_taps, lat_ext, lon_count):
    taps = jnp.transpose(filter_taps, (0, 2, 1, 3))
    output, field_grad, total = layer(features, cotangent, weight, taps, lat_ext, lon_count)
    cells = LATS * ROWS * LONS * WIDE
    output, field_grad, total = write(1.0 / math.sqrt(cells), output, field_grad, total)
    return (output, field_grad, total.reshape(BASES, CH, CH))


def solution(mesh):
    in_specs = (
        P("lat", "lon", None),
        P("lat", "lon", None),
        P(),
        P("lat", None, None, None),
        P("lat"),
        P("lat"),
    )
    out_specs = (P("lat", "lon", None), P("lat", "lon", None), P())
    return jax.shard_map(
        per_device, mesh=mesh, in_specs=in_specs, out_specs=out_specs, check_vma=False
    )
```

time: 62.2 us -> 50.7 us (0.82)
  Pallas kernels: 56.3 us -> 49.8 us
  local copies, waits for them, and re-layouts: 2.85 us -> 0 us
  other arithmetic: 2.15 us -> 0 us
    pallas_call x1 -> x2, Pallas kernels: 56.3 us -> 49.8 us  [the longest x1 48.7 us: layer(): pl.pallas_call(layer_kernel, out_shape=[pltpu.VMEM((ROWS, WIDE, CH), BF16...]
    unnamed x7 -> x0, local copies, waits for them, and re-layouts: 2.85 us -> none
    mul x1 -> x0, other arithmetic: 2.15 us -> none  [per_device(): total.astype(F32) * (1.0 / math.sqrt(cells))]
where the time goes in v3:
time: 50.7 us; the launch traced here: 50.5 us
  Pallas kernels  49.8 us (98%)
  between operations  0.64 us (1%)
    pallas_call x1, Pallas kernels, layer(): pl.pallas_call(layer_kernel, out_shape=[pltpu.VMEM((ROWS, WIDE, CH), BF16...  48.7 us
    pallas_call x1, Pallas kernels, write(): pl.pallas_call(lambda *refs: write_kernel(scale, *refs), out_shape=[jax.S...  1.09 us

profile of v3, /device:TPU:1, one launch (start us, length us, event | category | flops | bytes accessed | tf_op | source)
XLA Modules:
  0.0 50.5 jit_solution(7750117311222209235)
XLA Ops:
  0.6 48.7 %shard_map.85 = (bf16[4,32,256]{2,1,0:T(8,128)(2,1)S(1)}, bf16[4,32,256]{2,1,0:T(8,128)(2,1)S(1)}, bf16[2,32,16,256]{3,2,1,0:T(8,128)(2,1)S(1)}) custom-call(bf16[4,32,256]{2,1,0:T(8,128)(2,1)} %feat_any.1, bf16[4,32,256]{2,1,0:T(8,128)(2,1)} %cot_any.1, bf16[4,256,256]{2,1,0:T(8,128)(2,1)} %weight_any.1, bf16[4,5,4,64]{3,2,1,0:T(4,128)(2,1)} %bitcast.2, ...), custom_call_target="tpu_custom_call" | custom-call | tf_op jit(solution)/shard_map/pallas_call | solution.py:373
  49.4 1.1 %write.1 = (bf16[4,32,256]{2,1,0:T(8,128)(2,1)}, bf16[4,32,256]{2,1,0:T(8,128)(2,1)}, f32[2,32,16,256]{3,2,1,0:T(8,128)}) custom-call(bf16[4,32,256]{2,1,0:T(8,128)(2,1)S(1)} %get-tuple-element.9.refs_0_, bf16[4,32,256]{2,1,0:T(8,128)(2,1)S(1)} %get-tuple-element.10.refs_1_, bf16[2,32,16,256]{3,2,1,0:T(8,128)(2,1)S(1)} %get-tuple-element.11.refs_2_), custom_call_target="tpu_custom_call" | custom-call | tf_op jit(solution)/shard_map/write/pallas_call | solution.py:435

commit v4 on v3

--- a/solution.py
+++ b/solution.py
@@ -129,7 +129,7 @@
     fw, cw, weight_ref, ft, rt, bands, bo, bg, wedge, acc, part, pair_out, pair_in, half, group_in, zbuf,
     own_sem, feat_send, feat_recv, cot_send, cot_recv, ft_send, ft_recv, pair_send, pair_recv,
     group_send, group_recv, z_send, z_recv, all_send, all_recv, near_send, near_recv,
-    hop_sem, leap_sem,
+    hop_sem, leap_sem, step_sem, cross_sem, twin_sem,
 ):
     lat = lax.axis_index("lat")
     lon = lax.axis_index("lon")
@@ -143,12 +143,10 @@
     spot = (x * 4 + y_hi * 2 + y_lo) * 2 + z_lo
     partner = (lat + 1 - 2 * core, lon)
 
-    def group_device(index):
-        place = index // 2
-        return (
-            (place // 4) * 4 + (place % 2) * 2 + core,
-            ((place // 2) % 2) * ZLEN + z_hi * 2 + index % 2,
-        )
+    def across(dx, dy, dz):
+        far_x, far_y, far_z = (x + dx) % 4, (y_hi * 2 + y_lo + dy) % 4, (z_lo + dz) % 2
+        device = (far_x * 4 + (far_y % 2) * 2 + core, (far_y // 2) * ZLEN + z_hi * 2 + far_z)
+        return device, (far_x * 4 + far_y) * 2 + far_z
 
     def z_device(index):
         return (lat, y_hi * ZLEN + index)
@@ -159,7 +157,7 @@
     def beside(up, right):
         return ((lat + LATS + up) % LATS, (lon + LONS + right) % LONS)
 
-    ways = [(0, 1), (0, -1), (1, 1), (1, -1), (-1, 1), (-1, -1), (1, 0), (-1, 0)]
+    ways = [(1, 1), (1, -1), (-1, 1), (-1, -1), (0, 1), (0, -1), (1, 0), (-1, 0)]
 
     def remote(src, dst, send, recv, device):
         return pltpu.make_async_remote_copy(
@@ -167,21 +165,17 @@
             device_id=device, device_id_type=MESH,
         )
 
+    def signal(sem, device):
+        pl.semaphore_signal(sem, inc=1, device_id=device, device_id_type=MESH)
+
+    steps = [(1, 0), (3, 0), (0, 1), (0, 3)]
     barrier = pltpu.get_barrier_semaphore()
     for way in ways:
-        pl.semaphore_signal(barrier, inc=1, device_id=beside(*way), device_id_type=MESH)
-    pl.semaphore_signal(barrier, inc=1, device_id=z_device((z + 2) % ZLEN), device_id_type=MESH)
-    pl.semaphore_signal(
-        barrier, inc=1, device_id=z_device((z + ZLEN - 2) % ZLEN), device_id_type=MESH
-    )
-
-    def greet(step, carry):
-        pl.semaphore_signal(
-            barrier, inc=1, device_id=group_device((spot + step) % GROUP), device_id_type=MESH
-        )
-        return carry
-
-    lax.fori_loop(1, GROUP, greet, 0)
+        signal(barrier, beside(*way))
+    for dx, dy in steps:
+        signal(barrier, across(dx, dy, 0)[0])
+    signal(barrier, z_device((z + 2) % ZLEN))
+    signal(barrier, z_device((z + ZLEN - 2) % ZLEN))
 
     north = jnp.where(lat > 0, 1.0, 0.0)
     south = jnp.where(lat < LATS - 1, 1.0, 0.0)
@@ -194,14 +188,8 @@
     ]
     for copy in own_copies:
         copy.start()
-    blank = jnp.zeros((SPAN, LANES - 3 * WIDE, CH), BF16)
-    fw[:, 3 * WIDE :, :] = blank
-    cw[:, 3 * WIDE :, :] = blank
-    fill_filters(taps_ref, lat_ref, lon_ref, ft)
-    fill_forward(ft, north, south, bands)
     own_copies[0].wait()
-    own_copies[1].wait()
-    pl.semaphore_wait(barrier, len(ways) + 2 + (GROUP - 1))
+    pl.semaphore_wait(barrier, len(ways) + len(steps) + 2)
 
     def halo(window, send, recv):
         copies = []
@@ -225,15 +213,28 @@
     ]
     for copy in feat_copies:
         copy.start()
-    pl.semaphore_signal(hop_sem, inc=1, device_id=z_device((z + 2) % ZLEN), device_id_type=MESH)
-    pl.semaphore_signal(hop_sem, inc=1, device_id=z_device((z + ZLEN - 2) % ZLEN), device_id_type=MESH)
+    for dx, dy in steps:
+        signal(step_sem, across(dx, dy, 0)[0])
+    signal(hop_sem, z_device((z + 2) % ZLEN))
+    signal(hop_sem, z_device((z + ZLEN - 2) % ZLEN))
+    blank = jnp.zeros((SPAN, LANES - 3 * WIDE, CH), BF16)
+    fw[:, 3 * WIDE :, :] = blank
+    cw[:, 3 * WIDE :, :] = blank
+    fill_filters(taps_ref, lat_ref, lon_ref, ft)
+    fill_forward(ft, north, south, bands)
+    pl.semaphore_wait(step_sem, len(steps))
+    signal(cross_sem, across(2, 0, 0)[0])
+    signal(cross_sem, across(0, 2, 0)[0])
+    pl.semaphore_wait(hop_sem, 2)
+    signal(leap_sem, z_device((z + 4) % ZLEN))
+    signal(leap_sem, z_device((z + ZLEN - 4) % ZLEN))
+    pl.semaphore_wait(cross_sem, 2)
+    signal(twin_sem, across(0, 0, 1)[0])
     for copy in feat_copies:
         copy.wait_recv()
+    own_copies[1].wait()
     for copy in cot_copies + ft_copies:
         copy.start()
-    pl.semaphore_wait(hop_sem, 2)
-    pl.semaphore_signal(leap_sem, inc=1, device_id=z_device((z + 4) % ZLEN), device_id_type=MESH)
-    pl.semaphore_signal(leap_sem, inc=1, device_id=z_device((z + ZLEN - 4) % ZLEN), device_id_type=MESH)
     convolve(bands, fw, bo)
 
     cells = cw[inner, middle, :].reshape(ROWS * WIDE, CH)
@@ -257,28 +258,33 @@
         total = part[span, :] + pair_in[span, :].astype(F32)
         half[index * per : (index + 1) * per] = total.astype(BF16).reshape(per, CHUNK, CH)
 
+    offsets = [(dx, dy, dz) for dx in (0, 1, 2, 3) for dy in (0, 1, 2, 3) for dz in (0, 1)][1:]
+    offsets.sort(key=lambda o: -(min(o[0], 4 - o[0]) + min(o[1], 4 - o[1]) + o[2]))
+
     def group_copy(step):
-        target = (spot + step) % GROUP
+        device, piece = across(*offsets[step])
         return remote(
-            half.at[target], group_in.at[step], group_send.at[step], group_recv.at[step],
-            group_device(target),
-        )
-
-    def group_start(step, carry):
+            half.at[piece], group_in.at[step], group_send.at[step], group_recv.at[step], device
+        )
+
+    def group_slot(step):
+        return remote(
+            half.at[step], group_in.at[step], group_send.at[step], group_recv.at[step], partner
+        )
+
+    def group_add(step, carry):
+        group_slot(step).wait_recv()
+        return carry + group_in[step].astype(F32)
+
+    pl.semaphore_wait(twin_sem, 1)
+    for step in range(GROUP - 1):
         group_copy(step).start()
-        return carry
-
-    def group_add(step, carry):
-        group_copy(step).wait_recv()
-        return carry + group_in[step].astype(F32)
-
-    lax.fori_loop(1, GROUP, group_start, 0)
     own_copies[2].wait()
     mix(bo, weight_ref, out_ref)
     for copy in cot_copies + ft_copies:
         copy.wait_recv()
     fill_basis_grad(cw, weight_ref, bg)
-    chunk = lax.fori_loop(1, GROUP, group_add, half[spot].astype(F32))
+    chunk = lax.fori_loop(0, GROUP - 1, group_add, half[spot].astype(F32))
     zbuf[z_hi] = chunk.astype(BF16)
     pl.semaphore_wait(leap_sem, 2)
 
@@ -287,10 +293,6 @@
             zbuf.at[z_hi], zbuf.at[z_hi], z_send.at[step], z_recv.at[z_hi],
             far_device((z_hi + step) % ZFAR),
         )
-
-    def z_start(step, carry):
-        z_copy(step).start()
-        return carry
 
     def z_wait(step, carry):
         source = (z_hi + step) % ZFAR
@@ -299,7 +301,8 @@
         ).wait_recv()
         return carry
 
-    lax.fori_loop(1, ZFAR, z_start, 0)
+    for step in (4, 3, 5, 2, 6, 1, 7):
+        z_copy(step).start()
     fill_reversed(ft, north, south, rt)
     adjoint(rt, bg, wedge, acc, grad_ref)
     lax.fori_loop(1, ZFAR, z_wait, 0)
@@ -311,7 +314,7 @@
     def all_copy(step):
         return remote(
             sum_ref.at[core, spot], sum_ref.at[core, spot], all_send.at[step], all_recv.at[spot],
-            group_device((spot + step) % GROUP),
+            across(*offsets[step])[0],
         )
 
     def near_copy(index):
@@ -320,20 +323,17 @@
             near_recv.at[index], partner,
         )
 
-    def all_start(step, carry):
-        all_copy(step).start()
-        return carry
-
     def all_forward(step, carry):
         source = (spot + step) % GROUP
         remote(
             sum_ref.at[core, source], sum_ref.at[core, source], all_send.at[step],
-            all_recv.at[source], group_device(source),
+            all_recv.at[source], partner,
         ).wait_recv()
         near_copy(source).start()
         return carry
 
-    lax.fori_loop(1, GROUP, all_start, 0)
+    for step in range(GROUP - 1):
+        all_copy(step).start()
     near_copy(spot).start()
     for copy in feat_copies + cot_copies + ft_copies:
         copy.wait_send()
@@ -348,11 +348,14 @@
     lax.fori_loop(1, GROUP, all_forward, 0)
 
     def finish(step, carry):
-        group_copy(step).wait_send()
-        all_copy(step).wait_send()
-        return carry
-
-    lax.fori_loop(1, GROUP, finish, 0)
+        group_slot(step).wait_send()
+        remote(
+            sum_ref.at[core, spot], sum_ref.at[core, spot], all_send.at[step], all_recv.at[spot],
+            partner,
+        ).wait_send()
+        return carry
+
+    lax.fori_loop(0, GROUP - 1, finish, 0)
 
     def near_finish(index, carry):
         near_copy(index).wait_send()
@@ -400,7 +403,7 @@
             dma((8,)), dma((8,)), dma((8,)), dma((8,)), dma((2,)), dma((2,)), dma((2,)), dma((2,)),
             dma((GROUP,)), dma((GROUP,)), dma((ZFAR,)), dma((ZFAR,)),
             dma((GROUP,)), dma((GROUP,)), dma((GROUP,)), dma((GROUP,)),
-            pltpu.SemaphoreType.REGULAR, pltpu.SemaphoreType.REGULAR,
+            *[pltpu.SemaphoreType.REGULAR] * 5,
         ],
         compiler_params=pltpu.CompilerParams(collective_id=0, has_side_effects=True),
     )(features, cotangent, weight, filter_taps, lat_ext, lon_count)

time: 50.7 us -> 48 us (0.947)
  Pallas kernels: 49.8 us -> 47.1 us
    pallas_call x1, Pallas kernels: 48.7 us -> 46 us  [layer(): pl.pallas_call(layer_kernel, out_shape=[pltpu.VMEM((ROWS, WIDE, CH), BF16...]
where the time goes in v4:
time: 48 us; the launch traced here: 47.8 us
  Pallas kernels  47.1 us (98%)
  between operations  0.64 us (1%)
    pallas_call x1, Pallas kernels, layer(): pl.pallas_call(layer_kernel, out_shape=[pltpu.VMEM((ROWS, WIDE, CH), BF16...  46 us
    pallas_call x1, Pallas kernels, write(): pl.pallas_call(lambda *refs: write_kernel(scale, *refs), out_shape=[jax.S...  1.09 us

profile of v4, /device:TPU:1, one launch (start us, length us, event | category | flops | bytes accessed | tf_op | source)
XLA Modules:
  0.0 47.8 jit_solution(6469088454840412470)
XLA Ops:
  0.6 46.0 %shard_map.85 = (bf16[4,32,256]{2,1,0:T(8,128)(2,1)S(1)}, bf16[4,32,256]{2,1,0:T(8,128)(2,1)S(1)}, bf16[2,32,16,256]{3,2,1,0:T(8,128)(2,1)S(1)}) custom-call(bf16[4,32,256]{2,1,0:T(8,128)(2,1)} %feat_any.1, bf16[4,32,256]{2,1,0:T(8,128)(2,1)} %cot_any.1, bf16[4,256,256]{2,1,0:T(8,128)(2,1)} %weight_any.1, bf16[4,5,4,64]{3,2,1,0:T(4,128)(2,1)} %bitcast.2, ...), custom_call_target="tpu_custom_call" | custom-call | tf_op jit(solution)/shard_map/pallas_call | solution.py:376
  46.7 1.1 %write.1 = (bf16[4,32,256]{2,1,0:T(8,128)(2,1)}, bf16[4,32,256]{2,1,0:T(8,128)(2,1)}, f32[2,32,16,256]{3,2,1,0:T(8,128)}) custom-call(bf16[4,32,256]{2,1,0:T(8,128)(2,1)S(1)} %get-tuple-element.9.refs_0_, bf16[4,32,256]{2,1,0:T(8,128)(2,1)S(1)} %get-tuple-element.10.refs_1_, bf16[2,32,16,256]{3,2,1,0:T(8,128)(2,1)S(1)} %get-tuple-element.11.refs_2_), custom_call_target="tpu_custom_call" | custom-call | tf_op jit(solution)/shard_map/write/pallas_call | solution.py:438

commit v5 on v4

--- a/solution.py
+++ b/solution.py
@@ -124,11 +124,11 @@
 
 
 def layer_kernel(
-    feat_any, cot_any, weight_any, taps_ref, lat_ref, lon_ref,
+    feat_any, cot_any, weight_any, taps_any, lat_any, lon_any,
     out_ref, grad_ref, sum_ref,
-    fw, cw, weight_ref, ft, rt, bands, bo, bg, wedge, acc, part, pair_out, pair_in, half, group_in, zbuf,
+    fw, cw, weight_ref, taps_ref, lat_ref, lon_ref, ft, rt, bands, bo, bg, wedge, acc, part, pair_out, pair_in, half, group_in, zbuf,
     own_sem, feat_send, feat_recv, cot_send, cot_recv, ft_send, ft_recv, pair_send, pair_recv,
-    group_send, group_recv, z_send, z_recv, all_send, all_recv, near_send, near_recv,
+    group_recv, z_recv, all_recv, many_sem,
     hop_sem, leap_sem, step_sem, cross_sem, twin_sem,
 ):
     lat = lax.axis_index("lat")
@@ -185,28 +185,30 @@
         pltpu.make_async_copy(feat_any, fw.at[inner, middle], own_sem.at[0]),
         pltpu.make_async_copy(cot_any, cw.at[inner, middle], own_sem.at[1]),
         pltpu.make_async_copy(weight_any, weight_ref, own_sem.at[2]),
+        pltpu.make_async_copy(taps_any, taps_ref, own_sem.at[3]),
+        pltpu.make_async_copy(lat_any, lat_ref, own_sem.at[4]),
+        pltpu.make_async_copy(lon_any, lon_ref, own_sem.at[5]),
     ]
     for copy in own_copies:
         copy.start()
-    own_copies[0].wait()
     pl.semaphore_wait(barrier, len(ways) + len(steps) + 2)
 
-    def halo(window, send, recv):
+    def halo(source, window, send, recv):
         copies = []
         for index, (up, right) in enumerate(ways):
-            own = inner if up == 0 else slice(ROWS, ROWS + REACH) if up > 0 else slice(REACH, 2 * REACH)
+            own = slice(0, ROWS) if up == 0 else slice(ROWS - REACH, ROWS) if up > 0 else slice(0, REACH)
             line = inner if up == 0 else slice(0, REACH) if up > 0 else slice(REACH + ROWS, SPAN)
             left = WIDE * (1 - right)
             copies.append(
                 remote(
-                    window.at[own, middle], window.at[line, left : left + WIDE],
+                    source.at[own], window.at[line, left : left + WIDE],
                     send.at[index], recv.at[index], beside(up, right),
                 )
             )
         return copies
 
-    feat_copies = halo(fw, feat_send, feat_recv)
-    cot_copies = halo(cw, cot_send, cot_recv)
+    feat_copies = halo(feat_any, fw, feat_send, feat_recv)
+    cot_copies = halo(cot_any, cw, cot_send, cot_recv)
     ft_copies = [
         remote(ft.at[ROWS : ROWS + REACH], ft.at[0:REACH], ft_send.at[0], ft_recv.at[0], beside(1, 0)),
         remote(ft.at[REACH : 2 * REACH], ft.at[REACH + ROWS :], ft_send.at[1], ft_recv.at[1], beside(-1, 0)),
@@ -220,6 +222,8 @@
     blank = jnp.zeros((SPAN, LANES - 3 * WIDE, CH), BF16)
     fw[:, 3 * WIDE :, :] = blank
     cw[:, 3 * WIDE :, :] = blank
+    for copy in own_copies[3:]:
+        copy.wait()
     fill_filters(taps_ref, lat_ref, lon_ref, ft)
     fill_forward(ft, north, south, bands)
     pl.semaphore_wait(step_sem, len(steps))
@@ -228,10 +232,9 @@
     pl.semaphore_wait(hop_sem, 2)
     signal(leap_sem, z_device((z + 4) % ZLEN))
     signal(leap_sem, z_device((z + ZLEN - 4) % ZLEN))
-    pl.semaphore_wait(cross_sem, 2)
-    signal(twin_sem, across(0, 0, 1)[0])
     for copy in feat_copies:
         copy.wait_recv()
+    own_copies[0].wait()
     own_copies[1].wait()
     for copy in cot_copies + ft_copies:
         copy.start()
@@ -249,6 +252,8 @@
     for index in range(2):
         pair_out[index * CH : (index + 1) * CH, :] = share((1 - core) * 2 + index).astype(BF16)
         pair_copy(index).start()
+    pl.semaphore_wait(cross_sem, 2)
+    signal(twin_sem, across(0, 0, 1)[0])
     for index in range(2):
         part[index * CH : (index + 1) * CH, :] = share(core * 2 + index)
     per = GROUP // 2
@@ -264,12 +269,12 @@
     def group_copy(step):
         device, piece = across(*offsets[step])
         return remote(
-            half.at[piece], group_in.at[step], group_send.at[step], group_recv.at[step], device
+            half.at[piece], group_in.at[step], many_sem.at[0], group_recv.at[step], device
         )
 
     def group_slot(step):
         return remote(
-            half.at[step], group_in.at[step], group_send.at[step], group_recv.at[step], partner
+            half.at[step], group_in.at[step], many_sem.at[0], group_recv.at[step], partner
         )
 
     def group_add(step, carry):
@@ -281,28 +286,28 @@
         group_copy(step).start()
     own_copies[2].wait()
     mix(bo, weight_ref, out_ref)
+    chunk = lax.fori_loop(0, GROUP - 1, group_add, half[spot].astype(F32))
+    zbuf[z_hi] = chunk.astype(BF16)
+    pl.semaphore_wait(leap_sem, 2)
+
+    def z_copy(step):
+        return remote(
+            zbuf.at[z_hi], zbuf.at[z_hi], many_sem.at[1], z_recv.at[z_hi],
+            far_device((z_hi + step) % ZFAR),
+        )
+
+    def z_wait(step, carry):
+        source = (z_hi + step) % ZFAR
+        remote(
+            zbuf.at[source], zbuf.at[source], many_sem.at[1], z_recv.at[source], far_device(source)
+        ).wait_recv()
+        return carry
+
+    for step in (4, 3, 5, 2, 6, 1, 7):
+        z_copy(step).start()
     for copy in cot_copies + ft_copies:
         copy.wait_recv()
     fill_basis_grad(cw, weight_ref, bg)
-    chunk = lax.fori_loop(0, GROUP - 1, group_add, half[spot].astype(F32))
-    zbuf[z_hi] = chunk.astype(BF16)
-    pl.semaphore_wait(leap_sem, 2)
-
-    def z_copy(step):
-        return remote(
-            zbuf.at[z_hi], zbuf.at[z_hi], z_send.at[step], z_recv.at[z_hi],
-            far_device((z_hi + step) % ZFAR),
-        )
-
-    def z_wait(step, carry):
-        source = (z_hi + step) % ZFAR
-        remote(
-            zbuf.at[source], zbuf.at[source], z_send.at[step], z_recv.at[source], far_device(source)
-        ).wait_recv()
-        return carry
-
-    for step in (4, 3, 5, 2, 6, 1, 7):
-        z_copy(step).start()
     fill_reversed(ft, north, south, rt)
     adjoint(rt, bg, wedge, acc, grad_ref)
     lax.fori_loop(1, ZFAR, z_wait, 0)
@@ -313,24 +318,14 @@
 
     def all_copy(step):
         return remote(
-            sum_ref.at[core, spot], sum_ref.at[core, spot], all_send.at[step], all_recv.at[spot],
+            sum_ref.at[core, spot], sum_ref.at[core, spot], many_sem.at[2], all_recv.at[step],
             across(*offsets[step])[0],
         )
 
     def near_copy(index):
         return remote(
-            sum_ref.at[core, index], sum_ref.at[core, index], near_send.at[index],
-            near_recv.at[index], partner,
-        )
-
-    def all_forward(step, carry):
-        source = (spot + step) % GROUP
-        remote(
-            sum_ref.at[core, source], sum_ref.at[core, source], all_send.at[step],
-            all_recv.at[source], partner,
-        ).wait_recv()
-        near_copy(source).start()
-        return carry
+            sum_ref.at[core, index], sum_ref.at[core, index], many_sem.at[3], many_sem.at[4], partner
+        )
 
     for step in range(GROUP - 1):
         all_copy(step).start()
@@ -339,39 +334,34 @@
         copy.wait_send()
     for index in range(2):
         pair_copy(index).wait_send()
-
-    def z_finish(step, carry):
-        z_copy(step).wait_send()
-        return carry
-
-    lax.fori_loop(1, ZFAR, z_finish, 0)
-    lax.fori_loop(1, GROUP, all_forward, 0)
-
-    def finish(step, carry):
-        group_slot(step).wait_send()
+    remote(
+        half.at[0 : GROUP - 1], group_in.at[0 : GROUP - 1], many_sem.at[0], group_recv.at[0], partner
+    ).wait_send()
+    remote(
+        zbuf.at[0 : ZFAR - 1], zbuf.at[0 : ZFAR - 1], many_sem.at[1], z_recv.at[0], partner
+    ).wait_send()
+    for step in range(GROUP - 1):
+        dx, dy, dz = offsets[step]
+        source = across(4 - dx, 4 - dy, dz)[1]
         remote(
-            sum_ref.at[core, spot], sum_ref.at[core, spot], all_send.at[step], all_recv.at[spot],
+            sum_ref.at[core, source], sum_ref.at[core, source], many_sem.at[2], all_recv.at[step],
             partner,
-        ).wait_send()
-        return carry
-
-    lax.fori_loop(0, GROUP - 1, finish, 0)
-
-    def near_finish(index, carry):
-        near_copy(index).wait_send()
-        remote(
-            sum_ref.at[1 - core, index], sum_ref.at[1 - core, index], near_send.at[index],
-            near_recv.at[index], partner,
         ).wait_recv()
-        return carry
-
-    lax.fori_loop(0, GROUP, near_finish, 0)
+        near_copy(source).start()
+    remote(
+        sum_ref.at[core, 0 : GROUP - 1], sum_ref.at[core, 0 : GROUP - 1], many_sem.at[2],
+        all_recv.at[0], partner,
+    ).wait_send()
+    near_all = remote(
+        sum_ref.at[core], sum_ref.at[1 - core], many_sem.at[3], many_sem.at[4], partner
+    )
+    near_all.wait_send()
+    near_all.wait_recv()
 
 
 def layer(features, cotangent, weight, filter_taps, lat_ext, lon_count):
     dma = pltpu.SemaphoreType.DMA
     vmem = pl.BlockSpec(memory_space=pltpu.VMEM)
-    smem = pl.BlockSpec(memory_space=pltpu.SMEM)
     anywhere = pl.BlockSpec(memory_space=pl.ANY)
     return pl.pallas_call(
         layer_kernel,
@@ -380,12 +370,15 @@
             pltpu.VMEM((ROWS, WIDE, CH), BF16),
             pltpu.VMEM((2, GROUP, CHUNK, CH), BF16),
         ],
-        in_specs=[anywhere, anywhere, anywhere, vmem, smem, smem],
+        in_specs=[anywhere] * 6,
         out_specs=[vmem, vmem, vmem],
         scratch_shapes=[
             pltpu.VMEM((SPAN, LANES, CH), BF16),
             pltpu.VMEM((SPAN, LANES, CH), BF16),
             pltpu.VMEM((BASES, CH, CH), BF16),
+            pltpu.VMEM((ROWS, TAPS, BASES, 2 * HALF), BF16),
+            pltpu.SMEM((ROWS,), jnp.int32),
+            pltpu.SMEM((ROWS,), jnp.int32),
             pltpu.VMEM((SPAN, TAPS, 8, LANES), F32),
             pltpu.VMEM((SPAN, TAPS, 8, LANES), F32),
             pltpu.VMEM((ROWS, BASES * WIDE, TAPS * LANES), BF16),
@@ -399,10 +392,9 @@
             pltpu.VMEM((GROUP, CHUNK, CH), BF16),
             pltpu.VMEM((GROUP, CHUNK, CH), BF16),
             pltpu.VMEM((ZFAR, CHUNK, CH), BF16),
-            dma((3,)),
+            dma((6,)),
             dma((8,)), dma((8,)), dma((8,)), dma((8,)), dma((2,)), dma((2,)), dma((2,)), dma((2,)),
-            dma((GROUP,)), dma((GROUP,)), dma((ZFAR,)), dma((ZFAR,)),
-            dma((GROUP,)), dma((GROUP,)), dma((GROUP,)), dma((GROUP,)),
+            dma((GROUP,)), dma((ZFAR,)), dma((GROUP,)), dma((5,)),
             *[pltpu.SemaphoreType.REGULAR] * 5,
         ],
         compiler_params=pltpu.CompilerParams(collective_id=0, has_side_effects=True),

time: 48 us -> 46.4 us (0.967)
  Pallas kernels: 47.1 us -> 45.6 us
    pallas_call x1, Pallas kernels: 46 us -> 44.5 us  [layer(): pl.pallas_call(layer_kernel, out_shape=[pltpu.VMEM((ROWS, WIDE, CH), BF16...]
where the time goes in v5:
time: 46.4 us; the launch traced here: 46.2 us
  Pallas kernels  45.6 us (98%)
  between operations  0.64 us (1%)
    pallas_call x1, Pallas kernels, layer(): pl.pallas_call(layer_kernel, out_shape=[pltpu.VMEM((ROWS, WIDE, CH), BF16...  44.5 us
    pallas_call x1, Pallas kernels, write(): pl.pallas_call(lambda *refs: write_kernel(scale, *refs), out_shape=[jax.S...  1.09 us

profile of v5, /device:TPU:1, one launch (start us, length us, event | category | flops | bytes accessed | tf_op | source)
XLA Modules:
  0.0 46.2 jit_solution(12569518837680478847)
XLA Ops:
  0.6 44.5 %shard_map.85 = (bf16[4,32,256]{2,1,0:T(8,128)(2,1)S(1)}, bf16[4,32,256]{2,1,0:T(8,128)(2,1)S(1)}, bf16[2,32,16,256]{3,2,1,0:T(8,128)(2,1)S(1)}) custom-call(bf16[4,32,256]{2,1,0:T(8,128)(2,1)} %feat_any.1, bf16[4,32,256]{2,1,0:T(8,128)(2,1)} %cot_any.1, bf16[4,256,256]{2,1,0:T(8,128)(2,1)} %weight_any.1, bf16[4,5,4,64]{3,2,1,0:T(4,128)(2,1)} %bitcast.2, ...), custom_call_target="tpu_custom_call" | custom-call | tf_op jit(solution)/shard_map/pallas_call | solution.py:366
  45.1 1.1 %write.1 = (bf16[4,32,256]{2,1,0:T(8,128)(2,1)}, bf16[4,32,256]{2,1,0:T(8,128)(2,1)}, f32[2,32,16,256]{3,2,1,0:T(8,128)}) custom-call(bf16[4,32,256]{2,1,0:T(8,128)(2,1)S(1)} %get-tuple-element.9.refs_0_, bf16[4,32,256]{2,1,0:T(8,128)(2,1)S(1)} %get-tuple-element.10.refs_1_, bf16[2,32,16,256]{3,2,1,0:T(8,128)(2,1)S(1)} %get-tuple-element.11.refs_2_), custom_call_target="tpu_custom_call" | custom-call | tf_op jit(solution)/shard_map/write/pallas_call | solution.py:430

commit v6 on v5

--- a/solution.py
+++ b/solution.py
@@ -65,11 +65,12 @@
     lax.fori_loop(0, BASES, one, 0)
 
 
-def convolve(bands, fw, bo):
+def convolve(bands, fw, bo, first):
+    span = pl.ds(pl.multiple_of(first * WIDE, 2 * WIDE), 2 * WIDE)
     for row in range(ROWS):
         patch = fw[row : row + TAPS].reshape(TAPS * LANES, CH)
-        sums = jnp.dot(bands[row], patch, preferred_element_type=F32).astype(BF16)
-        bo[:, row * WIDE : (row + 1) * WIDE, :] = sums.reshape(BASES, WIDE, CH)
+        sums = jnp.dot(bands[row, span, :], patch, preferred_element_type=F32).astype(BF16)
+        bo[pl.ds(first, 2), row * WIDE : (row + 1) * WIDE, :] = sums.reshape(2, WIDE, CH)
 
 
 def mix(bo, weight_ref, out_ref):
@@ -140,13 +141,13 @@
     z_lo = z % 2
     z_hi = z // 2
     y_hi = lon // ZLEN
-    spot = (x * 4 + y_hi * 2 + y_lo) * 2 + z_lo
+    spot = z_lo * 16 + x * 4 + y_hi * 2 + y_lo
     partner = (lat + 1 - 2 * core, lon)
 
     def across(dx, dy, dz):
         far_x, far_y, far_z = (x + dx) % 4, (y_hi * 2 + y_lo + dy) % 4, (z_lo + dz) % 2
         device = (far_x * 4 + (far_y % 2) * 2 + core, (far_y // 2) * ZLEN + z_hi * 2 + far_z)
-        return device, (far_x * 4 + far_y) * 2 + far_z
+        return device, far_z * 16 + far_x * 4 + far_y
 
     def z_device(index):
         return (lat, y_hi * ZLEN + index)
@@ -157,7 +158,8 @@
     def beside(up, right):
         return ((lat + LATS + up) % LATS, (lon + LONS + right) % LONS)
 
-    ways = [(1, 1), (1, -1), (-1, 1), (-1, -1), (0, 1), (0, -1), (1, 0), (-1, 0)]
+    away = 2 * core - 1
+    ways = [(away, 1), (away, -1), (0, 1), (0, -1), (1, 0), (-1, 0)]
 
     def remote(src, dst, send, recv, device):
         return pltpu.make_async_remote_copy(
@@ -193,27 +195,46 @@
         copy.start()
     pl.semaphore_wait(barrier, len(ways) + len(steps) + 2)
 
+    def rows(window, start, left):
+        return window.at[pl.ds(start, REACH), left : left + WIDE]
+
+    common, single = REACH * (1 - core), REACH * core
+    far = REACH + ROWS
+
     def halo(source, window, send, recv):
-        copies = []
-        for index, (up, right) in enumerate(ways):
-            own = slice(0, ROWS) if up == 0 else slice(ROWS - REACH, ROWS) if up > 0 else slice(0, REACH)
-            line = inner if up == 0 else slice(0, REACH) if up > 0 else slice(REACH + ROWS, SPAN)
+        out, arrive = [], []
+
+        def add(src, start, landing, left, device):
+            index = len(out)
+            out.append(remote(src, rows(window, start, left), send.at[index], recv.at[index], device))
+            place = rows(window, landing, left)
+            arrive.append(remote(place, place, send.at[index], recv.at[index], partner))
+
+        for right in (1, -1):
+            start = REACH + common
+            add(source.at[pl.ds(common, REACH)], start, start, WIDE * (1 - right), beside(0, right))
+        for right in (1, -1):
+            add(
+                source.at[pl.ds(single, REACH)], far * (1 - core), far * core, WIDE * (1 - right),
+                beside(away, right),
+            )
+        for right in (1, -1):
+            start = REACH + single
+            add(source.at[pl.ds(single, REACH)], start, start, WIDE * (1 - right), beside(0, right))
+        add(source.at[ROWS - REACH :], 0, 0, WIDE, beside(1, 0))
+        add(source.at[0:REACH], far, far, WIDE, beside(-1, 0))
+        for right in (1, -1):
             left = WIDE * (1 - right)
-            copies.append(
-                remote(
-                    source.at[own], window.at[line, left : left + WIDE],
-                    send.at[index], recv.at[index], beside(up, right),
-                )
-            )
-        return copies
-
-    feat_copies = halo(feat_any, fw, feat_send, feat_recv)
-    cot_copies = halo(cot_any, cw, cot_send, cot_recv)
+            add(rows(window, REACH + common, left), far * core, far * (1 - core), left, partner)
+        return out, arrive
+
+    feat_copies, feat_arrive = halo(feat_any, fw, feat_send, feat_recv)
+    cot_copies, cot_arrive = halo(cot_any, cw, cot_send, cot_recv)
     ft_copies = [
         remote(ft.at[ROWS : ROWS + REACH], ft.at[0:REACH], ft_send.at[0], ft_recv.at[0], beside(1, 0)),
         remote(ft.at[REACH : 2 * REACH], ft.at[REACH + ROWS :], ft_send.at[1], ft_recv.at[1], beside(-1, 0)),
     ]
-    for copy in feat_copies:
+    for copy in feat_copies[:8]:
         copy.start()
     for dx, dy in steps:
         signal(step_sem, across(dx, dy, 0)[0])
@@ -232,13 +253,14 @@
     pl.semaphore_wait(hop_sem, 2)
     signal(leap_sem, z_device((z + 4) % ZLEN))
     signal(leap_sem, z_device((z + ZLEN - 4) % ZLEN))
-    for copy in feat_copies:
+    for index in range(2):
+        feat_arrive[index].wait_recv()
+        feat_copies[8 + index].start()
+    for copy in feat_arrive[2:]:
         copy.wait_recv()
     own_copies[0].wait()
     own_copies[1].wait()
-    for copy in cot_copies + ft_copies:
-        copy.start()
-    convolve(bands, fw, bo)
+    convolve(bands, fw, bo, (1 - core) * 2)
 
     cells = cw[inner, middle, :].reshape(ROWS * WIDE, CH)
 
@@ -254,39 +276,50 @@
         pair_copy(index).start()
     pl.semaphore_wait(cross_sem, 2)
     signal(twin_sem, across(0, 0, 1)[0])
+    convolve(bands, fw, bo, core * 2)
     for index in range(2):
         part[index * CH : (index + 1) * CH, :] = share(core * 2 + index)
     per = GROUP // 2
+    places = [(dx, dy) for dx in (0, 1, 2, 3) for dy in (0, 1, 2, 3)]
+    places.sort(key=lambda p: -(min(p[0], 4 - p[0]) + min(p[1], 4 - p[1])))
+    offsets = [(dx, dy, dz) for dx, dy in places for dz in (0, 1)]
+    offsets.sort(key=lambda o: -(min(o[0], 4 - o[0]) + min(o[1], 4 - o[1]) + o[2]))
+
+    def group_copy(index, dz):
+        device, piece = across(*places[index], dz)
+        slot = dz * per + index
+        return remote(half.at[piece], group_in.at[slot], many_sem.at[0], group_recv.at[slot], device)
+
+    def group_arrive(slot):
+        return remote(
+            group_in.at[slot], group_in.at[slot], many_sem.at[0], group_recv.at[slot], partner
+        )
+
+    def group_add(slot, carry):
+        group_arrive(slot).wait_recv()
+        return carry + group_in[slot].astype(F32)
+
     for index in range(2):
         pair_copy(index).wait_recv()
         span = slice(index * CH, (index + 1) * CH)
         total = part[span, :] + pair_in[span, :].astype(F32)
         half[index * per : (index + 1) * per] = total.astype(BF16).reshape(per, CHUNK, CH)
-
-    offsets = [(dx, dy, dz) for dx in (0, 1, 2, 3) for dy in (0, 1, 2, 3) for dz in (0, 1)][1:]
-    offsets.sort(key=lambda o: -(min(o[0], 4 - o[0]) + min(o[1], 4 - o[1]) + o[2]))
-
-    def group_copy(step):
-        device, piece = across(*offsets[step])
-        return remote(
-            half.at[piece], group_in.at[step], many_sem.at[0], group_recv.at[step], device
-        )
-
-    def group_slot(step):
-        return remote(
-            half.at[step], group_in.at[step], many_sem.at[0], group_recv.at[step], partner
-        )
-
-    def group_add(step, carry):
-        group_slot(step).wait_recv()
-        return carry + group_in[step].astype(F32)
-
-    pl.semaphore_wait(twin_sem, 1)
-    for step in range(GROUP - 1):
-        group_copy(step).start()
+        if index == 0:
+            pl.semaphore_wait(twin_sem, 1)
+        turn = (z_lo + index) % 2
+        for place in range(per - 1):
+            group_copy(place, turn).start()
+
+        @pl.when(turn == 1)
+        def _():
+            group_copy(per - 1, 1).start()
+
+    for copy in cot_copies[:8] + ft_copies:
+        copy.start()
     own_copies[2].wait()
     mix(bo, weight_ref, out_ref)
-    chunk = lax.fori_loop(0, GROUP - 1, group_add, half[spot].astype(F32))
+    chunk = lax.fori_loop(0, per - 1, group_add, half[spot].astype(F32))
+    chunk = lax.fori_loop(per, GROUP, group_add, chunk)
     zbuf[z_hi] = chunk.astype(BF16)
     pl.semaphore_wait(leap_sem, 2)
 
@@ -305,7 +338,10 @@
 
     for step in (4, 3, 5, 2, 6, 1, 7):
         z_copy(step).start()
-    for copy in cot_copies + ft_copies:
+    for index in range(2):
+        cot_arrive[index].wait_recv()
+        cot_copies[8 + index].start()
+    for copy in cot_arrive[2:] + ft_copies:
         copy.wait_recv()
     fill_basis_grad(cw, weight_ref, bg)
     fill_reversed(ft, north, south, rt)
@@ -393,7 +429,7 @@
             pltpu.VMEM((GROUP, CHUNK, CH), BF16),
             pltpu.VMEM((ZFAR, CHUNK, CH), BF16),
             dma((6,)),
-            dma((8,)), dma((8,)), dma((8,)), dma((8,)), dma((2,)), dma((2,)), dma((2,)), dma((2,)),
+            dma((10,)), dma((10,)), dma((10,)), dma((10,)), dma((2,)), dma((2,)), dma((2,)), dma((2,)),
             dma((GROUP,)), dma((ZFAR,)), dma((GROUP,)), dma((5,)),
             *[pltpu.SemaphoreType.REGULAR] * 5,
         ],

time: 46.4 us -> 46.3 us (level)
  no operation moved by 1% of the time
where the time goes in v6:
time: 46.3 us; the launch traced here: 46.1 us
  Pallas kernels  45.5 us (98%)
  between operations  0.64 us (1%)
    pallas_call x1, Pallas kernels, layer(): pl.pallas_call(layer_kernel, out_shape=[pltpu.VMEM((ROWS, WIDE, CH), BF16...  44.4 us
    pallas_call x1, Pallas kernels, write(): pl.pallas_call(lambda *refs: write_kernel(scale, *refs), out_shape=[jax.S...  1.09 us

profile of v6, /device:TPU:1, one launch (start us, length us, event | category | flops | bytes accessed | tf_op | source)
XLA Modules:
  0.0 46.1 jit_solution(7308323525548056577)
XLA Ops:
  0.6 44.4 %shard_map.85 = (bf16[4,32,256]{2,1,0:T(8,128)(2,1)S(1)}, bf16[4,32,256]{2,1,0:T(8,128)(2,1)S(1)}, bf16[2,32,16,256]{3,2,1,0:T(8,128)(2,1)S(1)}) custom-call(bf16[4,32,256]{2,1,0:T(8,128)(2,1)} %feat_any.1, bf16[4,32,256]{2,1,0:T(8,128)(2,1)} %cot_any.1, bf16[4,256,256]{2,1,0:T(8,128)(2,1)} %weight_any.1, bf16[4,5,4,64]{3,2,1,0:T(4,128)(2,1)} %bitcast.2, ...), custom_call_target="tpu_custom_call" | custom-call | tf_op jit(solution)/shard_map/pallas_call | solution.py:402
  45.1 1.1 %write.1 = (bf16[4,32,256]{2,1,0:T(8,128)(2,1)}, bf16[4,32,256]{2,1,0:T(8,128)(2,1)}, f32[2,32,16,256]{3,2,1,0:T(8,128)}) custom-call(bf16[4,32,256]{2,1,0:T(8,128)(2,1)S(1)} %get-tuple-element.9.refs_0_, bf16[4,32,256]{2,1,0:T(8,128)(2,1)S(1)} %get-tuple-element.10.refs_1_, bf16[2,32,16,256]{3,2,1,0:T(8,128)(2,1)S(1)} %get-tuple-element.11.refs_2_), custom_call_target="tpu_custom_call" | custom-call | tf_op jit(solution)/shard_map/write/pallas_call | solution.py:466

commit v7 on v6

--- a/solution.py
+++ b/solution.py
@@ -105,29 +105,29 @@
     rt[REACH + ROWS :] = rt[REACH + ROWS :] * south
 
 
-def adjoint(rt, bg, wedge, acc, grad_ref):
-    acc[...] = jnp.zeros((ROWS * WIDE, CH), F32)
-    for line in range(SPAN):
-        low, high = max(0, line - TAPS + 1), min(ROWS - 1, line)
-
-        def one(basis, carry):
-            start = pl.multiple_of(basis * LANES, LANES)
-            for row in range(low, high + 1):
-                tap = row + TAPS - 1 - line
+def fill_adjoint(rt, wedge):
+    def one(basis, carry):
+        for row in range(ROWS):
+            for tap in range(TAPS):
+                line = row + TAPS - 1 - tap
                 base = rt[line, tap, pl.ds(basis, 1), :]
+                start = pl.multiple_of((line * BASES + basis) * LANES, LANES)
                 wedge[row * WIDE : (row + 1) * WIDE, pl.ds(start, LANES)] = slanted(base).astype(BF16)
-            return carry
-
-        lax.fori_loop(0, BASES, one, 0)
-        span = slice(low * WIDE, (high + 1) * WIDE)
-        acc[span, :] = acc[span, :] + jnp.dot(wedge[span, :], bg[line], preferred_element_type=F32)
-    grad_ref[...] = acc[...].astype(BF16).reshape(ROWS, WIDE, CH)
+        return carry
+
+    lax.fori_loop(0, BASES, one, 0)
+
+
+def adjoint(wedge, bg, grad_ref):
+    flat = bg[...].reshape(SPAN * BASES * LANES, CH)
+    total = jnp.dot(wedge[...], flat, preferred_element_type=F32)
+    grad_ref[...] = total.astype(BF16).reshape(ROWS, WIDE, CH)
 
 
 def layer_kernel(
     feat_any, cot_any, weight_any, taps_any, lat_any, lon_any,
     out_ref, grad_ref, sum_ref,
-    fw, cw, weight_ref, taps_ref, lat_ref, lon_ref, ft, rt, bands, bo, bg, wedge, acc, part, pair_out, pair_in, half, group_in, zbuf,
+    fw, cw, weight_ref, taps_ref, lat_ref, lon_ref, ft, rt, bands, bo, bg, wedge, part, pair_out, pair_in, half, group_in, zbuf,
     own_sem, feat_send, feat_recv, cot_send, cot_recv, ft_send, ft_recv, pair_send, pair_recv,
     group_recv, z_recv, all_recv, many_sem,
     hop_sem, leap_sem, step_sem, cross_sem, twin_sem,
@@ -247,6 +247,7 @@
         copy.wait()
     fill_filters(taps_ref, lat_ref, lon_ref, ft)
     fill_forward(ft, north, south, bands)
+    wedge[...] = jnp.zeros(wedge.shape, BF16)
     pl.semaphore_wait(step_sem, len(steps))
     signal(cross_sem, across(2, 0, 0)[0])
     signal(cross_sem, across(0, 2, 0)[0])
@@ -338,14 +339,17 @@
 
     for step in (4, 3, 5, 2, 6, 1, 7):
         z_copy(step).start()
+    for copy in ft_copies:
+        copy.wait_recv()
     for index in range(2):
         cot_arrive[index].wait_recv()
         cot_copies[8 + index].start()
-    for copy in cot_arrive[2:] + ft_copies:
+    fill_reversed(ft, north, south, rt)
+    fill_adjoint(rt, wedge)
+    for copy in cot_arrive[2:]:
         copy.wait_recv()
     fill_basis_grad(cw, weight_ref, bg)
-    fill_reversed(ft, north, south, rt)
-    adjoint(rt, bg, wedge, acc, grad_ref)
+    adjoint(wedge, bg, grad_ref)
     lax.fori_loop(1, ZFAR, z_wait, 0)
     chunk = zbuf[0].astype(F32)
     for source in range(1, ZFAR):
@@ -420,8 +424,7 @@
             pltpu.VMEM((ROWS, BASES * WIDE, TAPS * LANES), BF16),
             pltpu.VMEM((BASES, ROWS * WIDE, CH), BF16),
             pltpu.VMEM((SPAN, BASES * LANES, CH), BF16),
-            pltpu.VMEM((ROWS * WIDE, BASES * LANES), BF16),
-            pltpu.VMEM((ROWS * WIDE, CH), F32),
+            pltpu.VMEM((ROWS * WIDE, SPAN * BASES * LANES), BF16),
             pltpu.VMEM((2 * CH, CH), F32),
             pltpu.VMEM((2 * CH, CH), BF16),
             pltpu.VMEM((2 * CH, CH), BF16),

time: 46.3 us -> 46.3 us (level)
  no operation moved by 1% of the time
where the time goes in v7:
time: 46.3 us; the launch traced here: 46.1 us
  Pallas kernels  45.5 us (98%)
  between operations  0.64 us (1%)
    pallas_call x1, Pallas kernels, layer(): pl.pallas_call(layer_kernel, out_shape=[pltpu.VMEM((ROWS, WIDE, CH), BF16...  44.4 us
    pallas_call x1, Pallas kernels, write(): pl.pallas_call(lambda *refs: write_kernel(scale, *refs), out_shape=[jax.S...  1.09 us

profile of v7, /device:TPU:1, one launch (start us, length us, event | category | flops | bytes accessed | tf_op | source)
XLA Modules:
  0.0 46.1 jit_solution(2214022903241680472)
XLA Ops:
  0.6 44.4 %shard_map.85 = (bf16[4,32,256]{2,1,0:T(8,128)(2,1)S(1)}, bf16[4,32,256]{2,1,0:T(8,128)(2,1)S(1)}, bf16[2,32,16,256]{3,2,1,0:T(8,128)(2,1)S(1)}) custom-call(bf16[4,32,256]{2,1,0:T(8,128)(2,1)} %feat_any.1, bf16[4,32,256]{2,1,0:T(8,128)(2,1)} %cot_any.1, bf16[4,256,256]{2,1,0:T(8,128)(2,1)} %weight_any.1, bf16[4,5,4,64]{3,2,1,0:T(4,128)(2,1)} %bitcast.2, ...), custom_call_target="tpu_custom_call" | custom-call | tf_op jit(solution)/shard_map/pallas_call | solution.py:406
  45.1 1.1 %write.1 = (bf16[4,32,256]{2,1,0:T(8,128)(2,1)}, bf16[4,32,256]{2,1,0:T(8,128)(2,1)}, f32[2,32,16,256]{3,2,1,0:T(8,128)}) custom-call(bf16[4,32,256]{2,1,0:T(8,128)(2,1)S(1)} %get-tuple-element.9.refs_0_, bf16[4,32,256]{2,1,0:T(8,128)(2,1)S(1)} %get-tuple-element.10.refs_1_, bf16[2,32,16,256]{3,2,1,0:T(8,128)(2,1)S(1)} %get-tuple-element.11.refs_2_), custom_call_target="tpu_custom_call" | custom-call | tf_op jit(solution)/shard_map/write/pallas_call | solution.py:469

commit v8 on v7

--- a/solution.py
+++ b/solution.py
@@ -275,6 +275,8 @@
     for index in range(2):
         pair_out[index * CH : (index + 1) * CH, :] = share((1 - core) * 2 + index).astype(BF16)
         pair_copy(index).start()
+    for copy in cot_copies[:8] + ft_copies:
+        copy.start()
     pl.semaphore_wait(cross_sem, 2)
     signal(twin_sem, across(0, 0, 1)[0])
     convolve(bands, fw, bo, core * 2)
@@ -315,8 +317,6 @@
         def _():
             group_copy(per - 1, 1).start()
 
-    for copy in cot_copies[:8] + ft_copies:
-        copy.start()
     own_copies[2].wait()
     mix(bo, weight_ref, out_ref)
     chunk = lax.fori_loop(0, per - 1, group_add, half[spot].astype(F32))

time: 46.3 us -> 46.2 us (level)
  no operation moved by 1% of the time
where the time goes in v8:
time: 46.2 us; the launch traced here: 46.1 us
  Pallas kernels  45.4 us (98%)
  between operations  0.64 us (1%)
    pallas_call x1, Pallas kernels, layer(): pl.pallas_call(layer_kernel, out_shape=[pltpu.VMEM((ROWS, WIDE, CH), BF16...  44.3 us
    pallas_call x1, Pallas kernels, write(): pl.pallas_call(lambda *refs: write_kernel(scale, *refs), out_shape=[jax.S...  1.09 us

profile of v8, /device:TPU:1, one launch (start us, length us, event | category | flops | bytes accessed | tf_op | source)
XLA Modules:
  0.0 46.1 jit_solution(9124485085513174312)
XLA Ops:
  0.6 44.3 %shard_map.85 = (bf16[4,32,256]{2,1,0:T(8,128)(2,1)S(1)}, bf16[4,32,256]{2,1,0:T(8,128)(2,1)S(1)}, bf16[2,32,16,256]{3,2,1,0:T(8,128)(2,1)S(1)}) custom-call(bf16[4,32,256]{2,1,0:T(8,128)(2,1)} %feat_any.1, bf16[4,32,256]{2,1,0:T(8,128)(2,1)} %cot_any.1, bf16[4,256,256]{2,1,0:T(8,128)(2,1)} %weight_any.1, bf16[4,5,4,64]{3,2,1,0:T(4,128)(2,1)} %bitcast.2, ...), custom_call_target="tpu_custom_call" | custom-call | tf_op jit(solution)/shard_map/pallas_call | solution.py:406
  45.0 1.1 %write.1 = (bf16[4,32,256]{2,1,0:T(8,128)(2,1)}, bf16[4,32,256]{2,1,0:T(8,128)(2,1)}, f32[2,32,16,256]{3,2,1,0:T(8,128)}) custom-call(bf16[4,32,256]{2,1,0:T(8,128)(2,1)S(1)} %get-tuple-element.9.refs_0_, bf16[4,32,256]{2,1,0:T(8,128)(2,1)S(1)} %get-tuple-element.10.refs_1_, bf16[2,32,16,256]{3,2,1,0:T(8,128)(2,1)S(1)} %get-tuple-element.11.refs_2_), custom_call_target="tpu_custom_call" | custom-call | tf_op jit(solution)/shard_map/write/pallas_call | solution.py:469

commit v9 on v7

--- a/solution.py
+++ b/solution.py
@@ -346,10 +346,6 @@
         cot_copies[8 + index].start()
     fill_reversed(ft, north, south, rt)
     fill_adjoint(rt, wedge)
-    for copy in cot_arrive[2:]:
-        copy.wait_recv()
-    fill_basis_grad(cw, weight_ref, bg)
-    adjoint(wedge, bg, grad_ref)
     lax.fori_loop(1, ZFAR, z_wait, 0)
     chunk = zbuf[0].astype(F32)
     for source in range(1, ZFAR):
@@ -370,6 +366,10 @@
     for step in range(GROUP - 1):
         all_copy(step).start()
     near_copy(spot).start()
+    for copy in cot_arrive[2:]:
+        copy.wait_recv()
+    fill_basis_grad(cw, weight_ref, bg)
+    adjoint(wedge, bg, grad_ref)
     for copy in feat_copies + cot_copies + ft_copies:
         copy.wait_send()
     for index in range(2):

time: 46.3 us -> 46.3 us (level)
  no operation moved by 1% of the time
where the time goes in v9:
time: 46.3 us; the launch traced here: 46.1 us
  Pallas kernels  45.5 us (98%)
  between operations  0.64 us (1%)
    pallas_call x1, Pallas kernels, layer(): pl.pallas_call(layer_kernel, out_shape=[pltpu.VMEM((ROWS, WIDE, CH), BF16...  44.4 us
    pallas_call x1, Pallas kernels, write(): pl.pallas_call(lambda *refs: write_kernel(scale, *refs), out_shape=[jax.S...  1.09 us

profile of v9, /device:TPU:1, one launch (start us, length us, event | category | flops | bytes accessed | tf_op | source)
XLA Modules:
  0.0 46.1 jit_solution(16106175929276161670)
XLA Ops:
  0.6 44.4 %shard_map.85 = (bf16[4,32,256]{2,1,0:T(8,128)(2,1)S(1)}, bf16[4,32,256]{2,1,0:T(8,128)(2,1)S(1)}, bf16[2,32,16,256]{3,2,1,0:T(8,128)(2,1)S(1)}) custom-call(bf16[4,32,256]{2,1,0:T(8,128)(2,1)} %feat_any.1, bf16[4,32,256]{2,1,0:T(8,128)(2,1)} %cot_any.1, bf16[4,256,256]{2,1,0:T(8,128)(2,1)} %weight_any.1, bf16[4,5,4,64]{3,2,1,0:T(4,128)(2,1)} %bitcast.2, ...), custom_call_target="tpu_custom_call" | custom-call | tf_op jit(solution)/shard_map/pallas_call | solution.py:406
  45.1 1.1 %write.1 = (bf16[4,32,256]{2,1,0:T(8,128)(2,1)}, bf16[4,32,256]{2,1,0:T(8,128)(2,1)}, f32[2,32,16,256]{3,2,1,0:T(8,128)}) custom-call(bf16[4,32,256]{2,1,0:T(8,128)(2,1)S(1)} %get-tuple-element.9.refs_0_, bf16[4,32,256]{2,1,0:T(8,128)(2,1)S(1)} %get-tuple-element.10.refs_1_, bf16[2,32,16,256]{3,2,1,0:T(8,128)(2,1)S(1)} %get-tuple-element.11.refs_2_), custom_call_target="tpu_custom_call" | custom-call | tf_op jit(solution)/shard_map/write/pallas_call | solution.py:469

commit v10 on v7

--- a/solution.py
+++ b/solution.py
@@ -356,10 +356,15 @@
         chunk = chunk + zbuf[source].astype(F32)
     sum_ref[core, spot] = chunk.astype(BF16)
 
-    def all_copy(step):
+    slots = {offset: step for step, offset in enumerate(offsets)}
+    feeders = {(3, 0, 0): [(2, dy, 0) for dy in (2, 1, 3, 0)], (0, 3, 0): [(dx, 2, 0) for dx in (1, 3, 0)]}
+    handed = feeders[3, 0, 0] + feeders[0, 3, 0]
+    direct = [o for o in offsets[: GROUP - 1] if o not in feeders and o not in handed]
+
+    def all_copy(piece, offset, device):
         return remote(
-            sum_ref.at[core, spot], sum_ref.at[core, spot], many_sem.at[2], all_recv.at[step],
-            across(*offsets[step])[0],
+            sum_ref.at[core, piece], sum_ref.at[core, piece], many_sem.at[2],
+            all_recv.at[slots[offset]], device,
         )
 
     def near_copy(index):
@@ -367,9 +372,17 @@
             sum_ref.at[core, index], sum_ref.at[core, index], many_sem.at[3], many_sem.at[4], partner
         )
 
-    for step in range(GROUP - 1):
-        all_copy(step).start()
+    for offset in list(feeders) + direct:
+        all_copy(spot, offset, across(*offset)[0]).start()
     near_copy(spot).start()
+    for offset in list(feeders) + direct + handed:
+        dx, dy, dz = offset
+        source = across(4 - dx, 4 - dy, dz)[1]
+        all_copy(source, offset, partner).wait_recv()
+        for goal in feeders.get(offset, []):
+            device = across((goal[0] - dx) % 4, (goal[1] - dy) % 4, 0)[0]
+            all_copy(source, goal, device).start()
+        near_copy(source).start()
     for copy in feat_copies + cot_copies + ft_copies:
         copy.wait_send()
     for index in range(2):
@@ -380,14 +393,6 @@
     remote(
         zbuf.at[0 : ZFAR - 1], zbuf.at[0 : ZFAR - 1], many_sem.at[1], z_recv.at[0], partner
     ).wait_send()
-    for step in range(GROUP - 1):
-        dx, dy, dz = offsets[step]
-        source = across(4 - dx, 4 - dy, dz)[1]
-        remote(
-            sum_ref.at[core, source], sum_ref.at[core, source], many_sem.at[2], all_recv.at[step],
-            partner,
-        ).wait_recv()
-        near_copy(source).start()
     remote(
         sum_ref.at[core, 0 : GROUP - 1], sum_ref.at[core, 0 : GROUP - 1], many_sem.at[2],
         all_recv.at[0], partner,

time: 46.3 us -> 47 us (1.015)
  Pallas kernels: 45.5 us -> 46.3 us
    pallas_call x1, Pallas kernels: 44.4 us -> 45.2 us  [layer(): pl.pallas_call(layer_kernel, out_shape=[pltpu.VMEM((ROWS, WIDE, CH), BF16...]
where the time goes in v10:
time: 47 us; the launch traced here: 46.9 us
  Pallas kernels  46.3 us (99%)
  between operations  0.64 us (1%)
    pallas_call x1, Pallas kernels, layer(): pl.pallas_call(layer_kernel, out_shape=[pltpu.VMEM((ROWS, WIDE, CH), BF16...  45.2 us
    pallas_call x1, Pallas kernels, write(): pl.pallas_call(lambda *refs: write_kernel(scale, *refs), out_shape=[jax.S...  1.09 us

profile of v10, /device:TPU:1, one launch (start us, length us, event | category | flops | bytes accessed | tf_op | source)
XLA Modules:
  0.0 46.9 jit_solution(10482467974857784459)
XLA Ops:
  0.6 45.2 %shard_map.85 = (bf16[4,32,256]{2,1,0:T(8,128)(2,1)S(1)}, bf16[4,32,256]{2,1,0:T(8,128)(2,1)S(1)}, bf16[2,32,16,256]{3,2,1,0:T(8,128)(2,1)S(1)}) custom-call(bf16[4,32,256]{2,1,0:T(8,128)(2,1)} %feat_any.1, bf16[4,32,256]{2,1,0:T(8,128)(2,1)} %cot_any.1, bf16[4,256,256]{2,1,0:T(8,128)(2,1)} %weight_any.1, bf16[4,5,4,64]{3,2,1,0:T(4,128)(2,1)} %bitcast.2, ...), custom_call_target="tpu_custom_call" | custom-call | tf_op jit(solution)/shard_map/pallas_call | solution.py:411
  45.8 1.1 %write.1 = (bf16[4,32,256]{2,1,0:T(8,128)(2,1)}, bf16[4,32,256]{2,1,0:T(8,128)(2,1)}, f32[2,32,16,256]{3,2,1,0:T(8,128)}) custom-call(bf16[4,32,256]{2,1,0:T(8,128)(2,1)S(1)} %get-tuple-element.9.refs_0_, bf16[4,32,256]{2,1,0:T(8,128)(2,1)S(1)} %get-tuple-element.10.refs_1_, bf16[2,32,16,256]{3,2,1,0:T(8,128)(2,1)S(1)} %get-tuple-element.11.refs_2_), custom_call_target="tpu_custom_call" | custom-call | tf_op jit(solution)/shard_map/write/pallas_call | solution.py:474

commit v11 on v7

--- a/solution.py
+++ b/solution.py
@@ -257,6 +257,8 @@
     for index in range(2):
         feat_arrive[index].wait_recv()
         feat_copies[8 + index].start()
+    pl.semaphore_wait(cross_sem, 2)
+    signal(twin_sem, across(0, 0, 1)[0])
     for copy in feat_arrive[2:]:
         copy.wait_recv()
     own_copies[0].wait()
@@ -275,8 +277,6 @@
     for index in range(2):
         pair_out[index * CH : (index + 1) * CH, :] = share((1 - core) * 2 + index).astype(BF16)
         pair_copy(index).start()
-    pl.semaphore_wait(cross_sem, 2)
-    signal(twin_sem, across(0, 0, 1)[0])
     convolve(bands, fw, bo, core * 2)
     for index in range(2):
         part[index * CH : (index + 1) * CH, :] = share(core * 2 + index)

time: 46.3 us -> 45.9 us (level)
  no operation moved by 1% of the time
where the time goes in v11:
time: 45.9 us; the launch traced here: 45.7 us
  Pallas kernels  45.1 us (98%)
  between operations  0.64 us (1%)
    pallas_call x1, Pallas kernels, layer(): pl.pallas_call(layer_kernel, out_shape=[pltpu.VMEM((ROWS, WIDE, CH), BF16...  44 us
    pallas_call x1, Pallas kernels, write(): pl.pallas_call(lambda *refs: write_kernel(scale, *refs), out_shape=[jax.S...  1.09 us

profile of v11, /device:TPU:1, one launch (start us, length us, event | category | flops | bytes accessed | tf_op | source)
XLA Modules:
  0.0 45.7 jit_solution(8262655672211405825)
XLA Ops:
  0.6 44.0 %shard_map.85 = (bf16[4,32,256]{2,1,0:T(8,128)(2,1)S(1)}, bf16[4,32,256]{2,1,0:T(8,128)(2,1)S(1)}, bf16[2,32,16,256]{3,2,1,0:T(8,128)(2,1)S(1)}) custom-call(bf16[4,32,256]{2,1,0:T(8,128)(2,1)} %feat_any.1, bf16[4,32,256]{2,1,0:T(8,128)(2,1)} %cot_any.1, bf16[4,256,256]{2,1,0:T(8,128)(2,1)} %weight_any.1, bf16[4,5,4,64]{3,2,1,0:T(4,128)(2,1)} %bitcast.2, ...), custom_call_target="tpu_custom_call" | custom-call | tf_op jit(solution)/shard_map/pallas_call | solution.py:406
  44.6 1.1 %write.1 = (bf16[4,32,256]{2,1,0:T(8,128)(2,1)}, bf16[4,32,256]{2,1,0:T(8,128)(2,1)}, f32[2,32,16,256]{3,2,1,0:T(8,128)}) custom-call(bf16[4,32,256]{2,1,0:T(8,128)(2,1)S(1)} %get-tuple-element.9.refs_0_, bf16[4,32,256]{2,1,0:T(8,128)(2,1)S(1)} %get-tuple-element.10.refs_1_, bf16[2,32,16,256]{3,2,1,0:T(8,128)(2,1)S(1)} %get-tuple-element.11.refs_2_), custom_call_target="tpu_custom_call" | custom-call | tf_op jit(solution)/shard_map/write/pallas_call | solution.py:469

commit v12 on v11

--- a/solution.py
+++ b/solution.py
@@ -246,14 +246,14 @@
     for copy in own_copies[3:]:
         copy.wait()
     fill_filters(taps_ref, lat_ref, lon_ref, ft)
-    fill_forward(ft, north, south, bands)
-    wedge[...] = jnp.zeros(wedge.shape, BF16)
     pl.semaphore_wait(step_sem, len(steps))
     signal(cross_sem, across(2, 0, 0)[0])
     signal(cross_sem, across(0, 2, 0)[0])
     pl.semaphore_wait(hop_sem, 2)
     signal(leap_sem, z_device((z + 4) % ZLEN))
     signal(leap_sem, z_device((z + ZLEN - 4) % ZLEN))
+    fill_forward(ft, north, south, bands)
+    wedge[...] = jnp.zeros(wedge.shape, BF16)
     for index in range(2):
         feat_arrive[index].wait_recv()
         feat_copies[8 + index].start()

time: 45.9 us -> 45.9 us (level)
  no operation moved by 1% of the time
where the time goes in v12:
time: 45.9 us; the launch traced here: 45.7 us
  Pallas kernels  45.1 us (98%)
  between operations  0.64 us (1%)
    pallas_call x1, Pallas kernels, layer(): pl.pallas_call(layer_kernel, out_shape=[pltpu.VMEM((ROWS, WIDE, CH), BF16...  44 us
    pallas_call x1, Pallas kernels, write(): pl.pallas_call(lambda *refs: write_kernel(scale, *refs), out_shape=[jax.S...  1.09 us

profile of v12, /device:TPU:1, one launch (start us, length us, event | category | flops | bytes accessed | tf_op | source)
XLA Modules:
  0.0 45.7 jit_solution(5598330644667570837)
XLA Ops:
  0.6 44.0 %shard_map.85 = (bf16[4,32,256]{2,1,0:T(8,128)(2,1)S(1)}, bf16[4,32,256]{2,1,0:T(8,128)(2,1)S(1)}, bf16[2,32,16,256]{3,2,1,0:T(8,128)(2,1)S(1)}) custom-call(bf16[4,32,256]{2,1,0:T(8,128)(2,1)} %feat_any.1, bf16[4,32,256]{2,1,0:T(8,128)(2,1)} %cot_any.1, bf16[4,256,256]{2,1,0:T(8,128)(2,1)} %weight_any.1, bf16[4,5,4,64]{3,2,1,0:T(4,128)(2,1)} %bitcast.2, ...), custom_call_target="tpu_custom_call" | custom-call | tf_op jit(solution)/shard_map/pallas_call | solution.py:406
  44.7 1.1 %write.1 = (bf16[4,32,256]{2,1,0:T(8,128)(2,1)}, bf16[4,32,256]{2,1,0:T(8,128)(2,1)}, f32[2,32,16,256]{3,2,1,0:T(8,128)}) custom-call(bf16[4,32,256]{2,1,0:T(8,128)(2,1)S(1)} %get-tuple-element.9.refs_0_, bf16[4,32,256]{2,1,0:T(8,128)(2,1)S(1)} %get-tuple-element.10.refs_1_, bf16[2,32,16,256]{3,2,1,0:T(8,128)(2,1)S(1)} %get-tuple-element.11.refs_2_), custom_call_target="tpu_custom_call" | custom-call | tf_op jit(solution)/shard_map/write/pallas_call | solution.py:469

commit v13 on v12

--- a/solution.py
+++ b/solution.py
@@ -317,8 +317,6 @@
 
     for copy in cot_copies[:8] + ft_copies:
         copy.start()
-    own_copies[2].wait()
-    mix(bo, weight_ref, out_ref)
     chunk = lax.fori_loop(0, per - 1, group_add, half[spot].astype(F32))
     chunk = lax.fori_loop(per, GROUP, group_add, chunk)
     zbuf[z_hi] = chunk.astype(BF16)
@@ -339,6 +337,8 @@
 
     for step in (4, 3, 5, 2, 6, 1, 7):
         z_copy(step).start()
+    own_copies[2].wait()
+    mix(bo, weight_ref, out_ref)
     for copy in ft_copies:
         copy.wait_recv()
     for index in range(2):

time: 45.9 us -> 45.9 us (level)
  no operation moved by 1% of the time
where the time goes in v13:
time: 45.9 us; the launch traced here: 45.7 us
  Pallas kernels  45.1 us (98%)
  between operations  0.64 us (1%)
    pallas_call x1, Pallas kernels, layer(): pl.pallas_call(layer_kernel, out_shape=[pltpu.VMEM((ROWS, WIDE, CH), BF16...  44 us
    pallas_call x1, Pallas kernels, write(): pl.pallas_call(lambda *refs: write_kernel(scale, *refs), out_shape=[jax.S...  1.09 us

profile of v13, /device:TPU:1, one launch (start us, length us, event | category | flops | bytes accessed | tf_op | source)
XLA Modules:
  0.0 45.7 jit_solution(18262239913226030700)
XLA Ops:
  0.6 44.0 %shard_map.85 = (bf16[4,32,256]{2,1,0:T(8,128)(2,1)S(1)}, bf16[4,32,256]{2,1,0:T(8,128)(2,1)S(1)}, bf16[2,32,16,256]{3,2,1,0:T(8,128)(2,1)S(1)}) custom-call(bf16[4,32,256]{2,1,0:T(8,128)(2,1)} %feat_any.1, bf16[4,32,256]{2,1,0:T(8,128)(2,1)} %cot_any.1, bf16[4,256,256]{2,1,0:T(8,128)(2,1)} %weight_any.1, bf16[4,5,4,64]{3,2,1,0:T(4,128)(2,1)} %bitcast.2, ...), custom_call_target="tpu_custom_call" | custom-call | tf_op jit(solution)/shard_map/pallas_call | solution.py:406
  44.7 1.1 %write.1 = (bf16[4,32,256]{2,1,0:T(8,128)(2,1)}, bf16[4,32,256]{2,1,0:T(8,128)(2,1)}, f32[2,32,16,256]{3,2,1,0:T(8,128)}) custom-call(bf16[4,32,256]{2,1,0:T(8,128)(2,1)S(1)} %get-tuple-element.9.refs_0_, bf16[4,32,256]{2,1,0:T(8,128)(2,1)S(1)} %get-tuple-element.10.refs_1_, bf16[2,32,16,256]{3,2,1,0:T(8,128)(2,1)S(1)} %get-tuple-element.11.refs_2_), custom_call_target="tpu_custom_call" | custom-call | tf_op jit(solution)/shard_map/write/pallas_call | solution.py:469
